TPU v7x, 128 devices: a whole 4x4x4 slice. The times are simulated.
128 devices in a mesh: rows: 16 (over z_lo, x, core), cols: 8 (over z_hi, y).
Axes of the slice: x: 4, y: 4, z: 4 (z_hi: 2, z_lo: 2; z = z_hi * 2 + z_lo), core: 2. Of those that a mesh axis runs over, the one named last changes fastest.
Arguments:
- spectrum: bfloat16 [2, 4096, 4096], P(None, 'rows', 'cols'), may hold values from -6 to 6
- diffraction: bfloat16 [2, 32, 3, 128, 128], P(None, 'rows'), may hold values from -0.21875 to 0.21875
- order_mask: int32 [32, 3], P('rows'), may hold values from 0 to 1, as said below
- phases: float32 [2, 4096, 4096], P(None, 'rows', 'cols'), may hold values from -3.140625 to 3.140625
- transmission: float32 [4096, 4096], P('rows', 'cols'), may hold values from 0.2 to 1
- shifts: int32 [2], replicated, may hold values from 128 to 256, as said below
Outputs:
- outgoing: float32 [2, 4096, 4096], P(None, 'rows', 'cols')
Inputs may be any that keep to these rules, and one draw needn't show every extreme that they name: Each bounce's shift lies between 128 and 256; one bounce shifts by exactly 256. `order_mask`: every block carries the orders -1 and +1; the order 0 is off in some blocks.
All inputs are finite; a program needn't handle non-finite values.
Results may differ from a plain program's by a relative error of at most 0.018.
Values may be sent and summed in bfloat16 or wider, within the bound.
A program may use at most 128 MiB of HBM per device.

v0:
```python
import math

import jax
import jax.numpy as jnp
from jax import lax
from jax.sharding import PartitionSpec as P

BLOCK = 128
BASE = 256
BOUNCES = 2


def shifted(value, axis, steps):
    count = lax.axis_size(axis)
    first, last = (max(0, -steps), min(count, count - steps))
    return lax.ppermute(value, axis, [(source, source + steps) for source in range(first, last)])


def twiddles(extent, sign_value, left_index, right_index):
    wrapped = left_index[:, None] * right_index[None, :] % extent
    angles = wrapped.astype(jnp.float32) * (2.0 * math.pi / extent)
    return (jnp.cos(angles), sign_value * jnp.sin(angles))


def base_tables(target, extent, sign_value):
    turn_real, turn_imag = twiddles(extent, sign_value, jnp.arange(BASE, dtype=jnp.int32), target)
    factor = 1.0 / math.sqrt(extent)
    return ((turn_real * factor).astype(jnp.bfloat16), (turn_imag * factor).astype(jnp.bfloat16))


def blocked_dft(values, axis_at, sign_value, target, extent):
    block_count = values.shape[axis_at] // BASE
    base_real, base_imag = base_tables(target, extent, sign_value)
    if axis_at == 1:
        shaped = values.reshape(2, block_count, BASE, values.shape[2])
        form_text = "sio,ik->sko"
    else:
        shaped = values.reshape(2, values.shape[1], block_count, BASE)
        form_text = "osi,ik->sok"

    def contract(left_side, right_side):
        return jnp.einsum(form_text, left_side, right_side, preferred_element_type=jnp.float32)

    inner_real = contract(shaped[0], base_real) - contract(shaped[1], base_imag)
    inner_imag = contract(shaped[0], base_imag) + contract(shaped[1], base_real)
    numbers = jnp.arange(block_count, dtype=jnp.int32) * BASE
    turn_real, turn_imag = twiddles(extent, sign_value, numbers, target)
    if axis_at == 1:
        turn_real = turn_real[:, :, None]
        turn_imag = turn_imag[:, :, None]
    else:
        turn_real = turn_real[:, None, :]
        turn_imag = turn_imag[:, None, :]
    out_real = jnp.sum(turn_real * inner_real - turn_imag * inner_imag, axis=0)
    out_imag = jnp.sum(turn_real * inner_imag + turn_imag * inner_real, axis=0)
    return jnp.stack([out_real, out_imag])


def apply_blocks(left_side, right_side):
    return jnp.einsum("bjk,bkq->bjq", left_side, right_side, preferred_element_type=jnp.float32)


def diffract(current, offset_step, matrices, weights):
    below_rows = shifted(current, "rows", 1)
    above_rows = shifted(current, "rows", -1)
    widened = jnp.concatenate([below_rows, current, above_rows], axis=1)
    height = current.shape[1]
    columns = current.shape[2]
    block_count = height // BLOCK
    result_real = jnp.zeros((block_count, BLOCK, columns), jnp.float32)
    result_imag = jnp.zeros((block_count, BLOCK, columns), jnp.float32)
    for order_at in range(3):
        source = lax.dynamic_slice_in_dim(widened, height + (order_at - 1) * offset_step, height, 1)
        source = source.reshape(2, block_count, BLOCK, columns)
        kernel = matrices[:, :, order_at]
        weight_now = weights[:, order_at][:, None, None]
        result_real = result_real + weight_now * (
            apply_blocks(kernel[0], source[0]) - apply_blocks(kernel[1], source[1])
        )
        result_imag = result_imag + weight_now * (
            apply_blocks(kernel[0], source[1]) + apply_blocks(kernel[1], source[0])
        )
    return (result_real.reshape(height, columns), result_imag.reshape(height, columns))


def on_device(spectrum, diffraction, order_mask, phases, transmission, shifts):
    local_rows = spectrum.shape[1]
    local_cols = spectrum.shape[2]
    row_count = lax.axis_size("rows")
    col_count = lax.axis_size("cols")
    full_rows = local_rows * row_count
    full_cols = local_cols * col_count
    own_rows = lax.axis_index("rows") * local_rows + jnp.arange(local_rows, dtype=jnp.int32)
    own_cols = lax.axis_index("cols") * local_cols + jnp.arange(local_cols, dtype=jnp.int32)
    weights = order_mask.astype(jnp.float32)

    def rows_gather(values, sign_value):
        summed = blocked_dft(
            lax.all_gather(values, "rows", axis=1, tiled=True), 1, sign_value, own_rows, full_rows
        )
        return summed.astype(jnp.bfloat16)

    def columns_gather(values, sign_value):
        return blocked_dft(
            lax.all_gather(values, "cols", axis=2, tiled=True), 2, sign_value, own_cols, full_cols
        )

    current = spectrum
    outgoing = None
    for bounce in range(BOUNCES):
        closing = bounce == BOUNCES - 1
        diff_real, diff_imag = diffract(current, shifts[bounce], diffraction, weights)
        cosine = jnp.cos(phases[bounce])
        sine_part = jnp.sin(phases[bounce])
        wave_k = jnp.stack(
            [diff_real * cosine - diff_imag * sine_part, diff_real * sine_part + diff_imag * cosine]
        ).astype(jnp.bfloat16)
        rows_space = rows_gather(wave_k, 1.0)
        space = columns_gather(rows_space, 1.0) * transmission[None]
        if closing:
            outgoing = space
        else:
            columns_k = columns_gather(space.astype(jnp.bfloat16), -1.0).astype(jnp.bfloat16)
            current = rows_gather(columns_k, -1.0)
    return outgoing


def solution(mesh):
    placed = (
        P(None, "rows", "cols"),
        P(None, "rows", None, None, None),
        P("rows", None),
        P(None, "rows", "cols"),
        P("rows", "cols"),
        P(),
    )
    return jax.shard_map(
        on_device, mesh=mesh, in_specs=placed, out_specs=P(None, "rows", "cols"), check_vma=False
    )
```

profile of v0, /device:TPU:1, one launch (start us, length us, event | category | flops | bytes accessed | tf_op | source)
XLA Modules:
  0.0 624.7 jit_solution(12232110755991861289)
XLA Ops:
  6.5 4.6 collective-permute-start
  24.1 2.0 fusion.57
  27.9 55.3 %all-gather.7.cloned.1.call-done = bf16[2,4096,512]{2,1,0:T(8,128)(2,1)} async-done(((bf16[2,256,512]{2,1,0:T(8,128)(2,1)}), bf16[2,4096,512]{2,1,0:T(8,128)(2,1)}) %all-gather.7.cloned.1.call-update) | async-done | bytes 8388624 | tf_op jit(solution)/shard_map/all_gather | solution.py:99
  83.2 3.8 fusion.317
  86.9 2.2 fusion.109
  89.2 2.3 fusion.119
  91.5 2.2 fusion.111
  93.7 6.7 %fusion.21 = (bf16[256,512]{1,0:T(8,128)(2,1)S(1)}, bf16[256,512]{1,0:T(8,128)(2,1)S(1)}) fusion(f32[16,256]{1,0:T(8,128)S(1)} %get-tuple-element.50, f32[16,256]{1,0:T(8,128)S(1)} %get-tuple-element.51, f32[256,16,512]{2,0,1:T(8,128)S(1)} %fusion.109, f32[256,16,512]{2,0,1:T(8,128)S(1)} %fusion.111, f32[256,16,512]{2,0,1:T(8,128)S(1)} %fusion.119, ...), kind=kOutput, calls=%fused_computation.43 | convolution fusion | flops 1095499776 | bytes 29918208 | tf_op jit(solution)/shard_map/sio,ik->sko/dot_general | solution.py:42
  102.7 75.1 %all-gather.9.cloned.1.call-done = bf16[2,256,4096]{2,1,0:T(8,128)(2,1)} async-done(((bf16[2,256,512]{2,1,0:T(8,128)(2,1)}), bf16[2,256,4096]{2,1,0:T(8,128)(2,1)}) %all-gather.9.cloned.1.call-update) | async-done | bytes 4194320 | tf_op jit(solution)/shard_map/all_gather | solution.py:105
  177.8 4.7 fusion.320
  182.5 3.3 copy.41
  185.7 5.4 fusion.80
  191.1 5.4 fusion.90
  196.5 3.3 copy.39
  199.8 3.1 fusion.82
  203.2 10.2 %fusion.17 = (f32[256,512]{0,1:T(8,128)S(1)}, f32[256,512]{0,1:T(8,128)S(1)}) fusion(f32[16,512]{1,0:T(8,128)S(1)} %get-tuple-element.47, f32[16,512]{1,0:T(8,128)S(1)} %get-tuple-element.48, f32[512,256,16]{1,0,2:T(8,128)} %fusion.80, f32[512,256,16]{1,0,2:T(8,128)S(1)} %fusion.82, f32[512,256,16]{1,0,2:T(8,128)S(1)} %copy-done.1, ...), kind=kOutput, calls=%fused_computation.35 | convolution fusion | flops 1096548352 | bytes 28379136 | tf_op jit(solution)/shard_map/osi,ik->sok/dot_general | solution.py:42
  214.8 70.6 %all-gather.11.cloned.1.call-done = bf16[2,256,4096]{1,2,0:T(8,128)(2,1)} async-done(((bf16[2,256,512]{1,2,0:T(8,128)(2,1)}), bf16[2,256,4096]{1,2,0:T(8,128)(2,1)}) %all-gather.11.cloned.1.call-update) | async-done | bytes 4194320 | tf_op jit(solution)/shard_map/all_gather | solution.py:105
  285.4 2.5 fusion.319
  287.9 3.1 fusion.76
  291.0 3.2 fusion.94
  294.2 3.1 fusion.78
  297.3 8.7 %fusion.13 = (bf16[256,512]{0,1:T(8,128)(2,1)S(1)}, bf16[256,512]{0,1:T(8,128)(2,1)S(1)}) fusion(f32[16,512]{1,0:T(8,128)S(1)} %get-tuple-element.46, f32[16,512]{1,0:T(8,128)S(1)} %get-tuple-element.48, f32[512,256,16]{1,0,2:T(8,128)S(1)} %fusion.76, f32[512,256,16]{1,0,2:T(8,128)S(1)} %fusion.78, f32[512,256,16]{1,0,2:T(8,128)S(1)} %fusion.94, ...), kind=kOutput, calls=%fused_computation.27 | convolution fusion | flops 1096548352 | bytes 27854848 | tf_op jit(solution)/shard_map/osi,ik->sok/dot_general | solution.py:42
  307.1 59.8 %all-gather.13.cloned.1.call-done = bf16[2,4096,512]{1,2,0:T(8,128)(2,1)} async-done(((bf16[2,256,512]{1,2,0:T(8,128)(2,1)}), bf16[2,4096,512]{1,2,0:T(8,128)(2,1)}) %all-gather.13.cloned.1.call-update) | async-done | bytes 8388624 | tf_op jit(solution)/shard_map/all_gather | solution.py:99
  366.9 6.0 fusion.316
  372.9 6.5 %copy.51 = bf16[1,4096,512]{2,1,0:T(8,128)(2,1)} copy(bf16[1,4096,512]{1,2,0:T(8,128)(2,1)} %get-tuple-element.22) | data formatting | bytes 8388608 | tf_op jit(solution)/shard_map/slice | solution.py:44
  379.3 7.8 %fusion.105 = f32[256,16,512]{2,0,1:T(8,128)} fusion(bf16[16,256,512]{2,1,0:T(8,128)(2,1)} %bitcast.390, s32[256]{0:T(256)S(1)} %copy-done.12), kind=kOutput, calls=%fused_computation.166 | convolution fusion | flops 1074790400 | bytes 12583936 | tf_op jit(solution)/shard_map/sio,ik->sko/dot_general | solution.py:42
  387.2 5.5 fusion.123
  392.6 6.5 %copy.50 = bf16[1,4096,512]{2,1,0:T(8,128)(2,1)} copy(bf16[1,4096,512]{1,2,0:T(8,128)(2,1)} %get-tuple-element.23) | data formatting | bytes 8388608 | tf_op jit(solution)/shard_map/slice | solution.py:44
  399.2 4.6 fusion.107
  405.1 8.0 %fusion.9 = (bf16[256,512]{1,0:T(8,128)(2,1)S(1)}, bf16[256,512]{1,0:T(8,128)(2,1)S(1)}) fusion(f32[16,256]{1,0:T(8,128)S(1)} %copy-done.15, f32[16,256]{1,0:T(8,128)S(1)} %get-tuple-element.51, f32[256,16,512]{2,0,1:T(8,128)} %fusion.105, f32[256,16,512]{2,0,1:T(8,128)S(1)} %fusion.107, f32[256,16,512]{2,0,1:T(8,128)S(1)} %copy-done.4, ...), kind=kOutput, calls=%fused_computation.19 | convolution fusion | flops 1095499776 | bytes 29918208 | tf_op jit(solution)/shard_map/sio,ik->sko/dot_general | solution.py:42
  413.1 2.2 collective-permute-start.3
  415.3 3.4 collective-permute-start.2
  421.0 2.6 collective-permute-done.3
  428.7 2.1 fusion.53
  432.0 53.6 %all-gather.15.cloned.1.call-done = bf16[2,4096,512]{2,1,0:T(8,128)(2,1)} async-done(((bf16[2,256,512]{2,1,0:T(8,128)(2,1)}), bf16[2,4096,512]{2,1,0:T(8,128)(2,1)}) %all-gather.15.cloned.1.call-update) | async-done | bytes 8388624 | tf_op jit(solution)/shard_map/all_gather | solution.py:99
  485.6 3.8 fusion.315
  489.3 2.2 fusion.101
  491.6 2.3 fusion.115
  493.8 2.2 fusion.103
  496.1 6.7 %fusion.5 = (bf16[256,512]{1,0:T(8,128)(2,1)S(1)}, bf16[256,512]{1,0:T(8,128)(2,1)S(1)}) fusion(f32[16,256]{1,0:T(8,128)S(1)} %copy-done.14, f32[16,256]{1,0:T(8,128)S(1)} %get-tuple-element.51, f32[256,16,512]{2,0,1:T(8,128)S(1)} %fusion.101, f32[256,16,512]{2,0,1:T(8,128)S(1)} %fusion.103, f32[256,16,512]{2,0,1:T(8,128)S(1)} %fusion.115, ...), kind=kOutput, calls=%fused_computation.11 | convolution fusion | flops 1095499776 | bytes 29918208 | tf_op jit(solution)/shard_map/sio,ik->sko/dot_general | solution.py:42
  503.6 76.5 %all-gather.17.cloned.1.call-done = bf16[2,256,4096]{2,1,0:T(8,128)(2,1)} async-done(((bf16[2,256,512]{2,1,0:T(8,128)(2,1)}), bf16[2,256,4096]{2,1,0:T(8,128)(2,1)}) %all-gather.17.cloned.1.call-update) | async-done | bytes 4194320 | tf_op jit(solution)/shard_map/all_gather | solution.py:105
  580.1 4.7 fusion.318
  584.8 3.3 copy.54
  588.1 5.4 fusion.72
  593.4 5.4 fusion.86
  598.8 3.5 copy.52
  602.4 3.1 fusion.74
  605.7 10.2 %fusion.1 = (f32[256,512]{0,1:T(8,128)S(1)}, f32[256,512]{0,1:T(8,128)S(1)}) fusion(f32[16,512]{1,0:T(8,128)S(1)} %get-tuple-element.47, f32[16,512]{1,0:T(8,128)S(1)} %get-tuple-element.48, f32[512,256,16]{1,0,2:T(8,128)} %fusion.72, f32[512,256,16]{1,0,2:T(8,128)S(1)} %fusion.74, f32[512,256,16]{1,0,2:T(8,128)S(1)} %copy-done, ...), kind=kOutput, calls=%fused_computation.3 | convolution fusion | flops 1096548352 | bytes 28379136 | tf_op jit(solution)/shard_map/osi,ik->sok/dot_general | solution.py:42
  (111 shorter events, 27.8 us)
Async XLA Ops:
  6.5 15.4 %copy-start.6 = (bf16[2,256,512]{2,1,0:T(8,128)(2,1)S(1)}, bf16[2,256,512]{2,1,0:T(8,128)(2,1)}, u32[]{:S(2)}) copy-start(bf16[2,256,512]{2,1,0:T(8,128)(2,1)} %param.6) | copy-start | bytes 1572868
  6.5 15.1 %copy-start.5 = (bf16[2,2,3,128,128]{4,3,2,1,0:T(8,128)(2,1)S(1)}, bf16[2,2,3,128,128]{4,3,2,1,0:T(8,128)(2,1)}, u32[]{:S(2)}) copy-start(bf16[2,2,3,128,128]{4,3,2,1,0:T(8,128)(2,1)} %param.7) | copy-start | bytes 1179652
  6.5 76.6 %all-gather.7.cloned.1.call-start = ((), (), s32[]{:S(2)}) async-start(), calls=%async_computation | async-start | bytes 8912896 | tf_op jit(solution)/shard_map/all_gather | solution.py:99
  6.5 15.3 %collective-permute-start = (bf16[2,256,512]{2,1,0:T(8,128)(2,1)}, bf16[2,256,512]{2,1,0:T(8,128)(2,1)S(1)}, u32[]{:S(2)}, u32[]{:S(2)}) collective-permute-start(bf16[2,256,512]{2,1,0:T(8,128)(2,1)} %param.6), channel_id=1, source_target_pairs={{0,8},{8,16},{16,24},{24,32},{32,40},{40,48},{48,56},{56,64},{64,7... | collective-permute-start | bytes 1572872 | tf_op jit(solution)/shard_map/ppermute | solution.py:16
  11.2 10.8 %collective-permute-start.1 = (bf16[2,256,512]{2,1,0:T(8,128)(2,1)}, bf16[2,256,512]{2,1,0:T(8,128)(2,1)S(1)}, u32[]{:S(2)}, u32[]{:S(2)}) collective-permute-start(bf16[2,256,512]{2,1,0:T(8,128)(2,1)} %param.6), channel_id=1, source_target_pairs={{8,0},{16,8},{24,16},{32,24},{40,32},{48,40},{56,48},{64,56},{72,6... | collective-permute-start | bytes 1572872 | tf_op jit(solution)/shard_map/ppermute | solution.py:16
  15.1 7.2 %copy-start.16 = (f32[2]{0:T(128)}, f32[2]{0:T(128)S(1)}, u32[]{:S(2)}) copy-start(f32[2]{0:T(128)S(1)} %get-tuple-element.18) | copy-start | bytes 28
  15.1 8.3 %copy-start.18 = (f32[2]{0:T(128)}, f32[2]{0:T(128)S(1)}, u32[]{:S(2)}) copy-start(f32[2]{0:T(128)S(1)} %get-tuple-element.19) | copy-start | bytes 28
  15.1 8.8 %copy-start.20 = (f32[2]{0:T(128)}, f32[2]{0:T(128)S(1)}, u32[]{:S(2)}) copy-start(f32[2]{0:T(128)S(1)} %get-tuple-element.17) | copy-start | bytes 28
  22.9 1.2 copy-start.7
  27.0 150.8 %all-gather.9.cloned.1.call-start = ((), (), s32[]{:S(2)}) async-start(), calls=%async_computation.1 | async-start | bytes 4718592 | tf_op jit(solution)/shard_map/all_gather | solution.py:105
  27.1 59.9 %copy-start.22 = (s32[16]{0:T(128)}, s32[16]{0:T(128)S(1)}, u32[]{:S(2)}) copy-start(s32[16]{0:T(128)S(1)} %iota_multiply_fusion) | copy-start | bytes 196
  27.1 66.6 %copy-start.11 = (s32[256]{0:T(256)}, s32[256]{0:T(256)S(1)}, u32[]{:S(2)}) copy-start(s32[256]{0:T(256)S(1)} %iota_add_fusion.1) | copy-start | bytes 3076
  27.9 65.8 %copy-start.13 = (f32[16,256]{1,0:T(8,128)}, f32[16,256]{1,0:T(8,128)S(1)}, u32[]{:S(2)}) copy-start(f32[16,256]{1,0:T(8,128)S(1)} %get-tuple-element.50) | copy-start | bytes 49156
  93.7 7.9 %copy-start.9 = (f32[256,512]{1,0:T(8,128)S(1)}, f32[256,512]{1,0:T(8,128)}, u32[]{:S(2)}) copy-start(f32[256,512]{1,0:T(8,128)} %param.10) | copy-start | bytes 1572868
  101.3 184.1 %all-gather.11.cloned.1.call-start = ((), (), s32[]{:S(2)}) async-start(), calls=%async_computation.2 | async-start | bytes 4718592 | tf_op jit(solution)/shard_map/all_gather | solution.py:105
  199.8 3.4 copy-start.1
  214.4 152.5 %all-gather.13.cloned.1.call-start = ((), (), s32[]{:S(2)}) async-start(), calls=%async_computation.3 | async-start | bytes 8912896 | tf_op jit(solution)/shard_map/all_gather | solution.py:99
  306.9 178.7 %all-gather.15.cloned.1.call-start = ((), (), s32[]{:S(2)}) async-start(), calls=%async_computation.4 | async-start | bytes 8912896 | tf_op jit(solution)/shard_map/all_gather | solution.py:99
  372.9 6.5 %copy-start.12 = (s32[256]{0:T(256)S(1)}, s32[256]{0:T(256)}, u32[]{:S(2)}) copy-start(s32[256]{0:T(256)} %copy-done.11) | copy-start | bytes 3076
  379.3 7.8 %copy-start.2 = (bf16[1,4096,512]{2,1,0:T(8,128)(2,1)S(1)}, bf16[1,4096,512]{2,1,0:T(8,128)(2,1)}, u32[]{:S(2)}) copy-start(bf16[1,4096,512]{2,1,0:T(8,128)(2,1)} %copy.51) | copy-start | bytes 12582916
  392.6 11.1 %copy-start.15 = (f32[16,256]{1,0:T(8,128)S(1)}, f32[16,256]{1,0:T(8,128)}, u32[]{:S(2)}) copy-start(f32[16,256]{1,0:T(8,128)} %get-tuple-element.49) | copy-start | bytes 49156
  399.2 4.6 copy-start.3
  399.2 5.9 copy-start.4
  413.1 10.5 %collective-permute-start.3 = (bf16[2,256,512]{2,1,0:T(8,128)(2,1)S(1)}, bf16[2,256,512]{2,1,0:T(8,128)(2,1)S(1)}, u32[]{:S(2)}, u32[]{:S(2)}) collective-permute-start(bf16[2,256,512]{2,1,0:T(8,128)(2,1)S(1)} %pad_maximum_fusion.4), channel_id=1, source_target_pairs={{8,0},{16,8},{24,16},{32,24},{40,32},{48,40},{56,48},{64,56},{72,6... | collective-permute-start | bytes 1572872 | tf_op jit(solution)/shard_map/ppermute | solution.py:16
  415.3 9.5 %collective-permute-start.2 = (bf16[2,256,512]{2,1,0:T(8,128)(2,1)S(1)}, bf16[2,256,512]{2,1,0:T(8,128)(2,1)}, u32[]{:S(2)}, u32[]{:S(2)}) collective-permute-start(bf16[2,256,512]{2,1,0:T(8,128)(2,1)S(1)} %pad_maximum_fusion.4), channel_id=1, source_target_pairs={{0,8},{8,16},{16,24},{24,32},{32,40},{40,48},{48,56},{56,64},{64,7... | collective-permute-start | bytes 1572872 | tf_op jit(solution)/shard_map/ppermute | solution.py:16
  420.6 6.2 copy-start.19
  423.6 0.8 copy-start.10
  426.1 1.6 copy-start.17
  426.4 1.6 copy-start.21
  427.5 1.2 copy-start.8
  431.7 148.4 %all-gather.17.cloned.1.call-start = ((), (), s32[]{:S(2)}) async-start(), calls=%async_computation.5 | async-start | bytes 4718592 | tf_op jit(solution)/shard_map/all_gather | solution.py:105
  493.8 2.3 copy-start.14
  602.4 3.4 copy-start
Sparse Core Ops, SparseCore 0:
  27.1 55.9 all-gather.6
  101.4 76.3 all-gather.8
  214.5 70.8 all-gather.10
  307.0 59.8 all-gather.12
  431.8 53.6 all-gather.14
  503.8 76.3 all-gather.16
where the time goes:
time: 635 us; the launch traced here: 625 us
  waiting for transfers between devices  394 us (62%)
  matrix products  127 us (20%)
  local copies, waits for them, and re-layouts  59.3 us (9%)
  between operations  18.5 us (3%)
  starting transfers between devices  13.3 us (2%)
  other arithmetic  13 us (2%)
    all_gather x3, waiting for transfers between devices, columns_gather(): lax.all_gather(values, 'cols', axis=2, tiled=True)  222 us
    all_gather x3, waiting for transfers between devices, rows_gather(): lax.all_gather(values, 'rows', axis=1, tiled=True)  169 us
    dot_general x24, matrix products, contract(): jnp.einsum(form_text, left_side, right_side, preferred_element_type=jnp.f...  119 us
    slice x12, local copies, waits for them, and re-layouts, blocked_dft(): inner_real = contract(shaped[0], base_real) - contract(shaped[1], base_imag)  51.6 us
  transfers between devices with their start and end apart: 10, of which 8 were waited for; matrix products, arithmetic and copies ran while one was open for 1% of the time, Pallas kernels for 0%

commit v1 on v0

v1 whole, which is shorter than its diff:
```python
import math

import jax
import jax.numpy as jnp
import numpy as np
from jax import lax
from jax.experimental import pallas as pl
from jax.experimental.pallas import tpu as pltpu
from jax.sharding import PartitionSpec as P

F32 = jnp.float32
BF16 = jnp.bfloat16
NR = 16
NC = 8
FULL = 4096


def tables():
    def circle(count, rows, columns):
        angle = 2.0 * np.pi * ((np.arange(rows)[:, None] * np.arange(columns)[None, :]) % count) / count
        return np.cos(angle), np.sin(angle)

    c256, s256 = circle(256, 256, 256)
    c512, s512 = circle(512, 512, 512)
    base_rows = np.stack([c256, s256]) / 64.0
    base_cols = np.stack([c512, s512]) / 64.0
    turn_rows = np.stack(circle(FULL, NR, 256))[:, :, None, :]
    turn_cols = np.stack(circle(FULL, NC, 512))[:, :, None, :]
    return (
        jnp.asarray(base_rows, BF16),
        jnp.asarray(base_cols, BF16),
        jnp.asarray(turn_rows, F32),
        jnp.asarray(turn_cols, F32),
    )


def times_unit(value, numerator, count, sign):
    real, imag = value
    step = (numerator * 8) % (count * 8)
    eighth, rest = divmod(step, count)
    if rest == 0 and eighth % 2 == 0:
        quarter = (eighth // 2) % 4
        if quarter == 0:
            return real, imag
        if quarter == 2:
            return -real, -imag
        if (quarter == 1) == (sign > 0):
            return -imag, real
        return imag, -real
    angle = 2.0 * math.pi * numerator / count
    cosine, sine = math.cos(angle), sign * math.sin(angle)
    if rest == 0:
        half = abs(cosine)
        a = (real - imag) if cosine * sine > 0 else (real + imag)
        b = (real + imag) if cosine * sine > 0 else (imag - real)
        if cosine < 0:
            return a * (-half), b * (-half)
        return a * half, b * half
    return real * cosine - imag * sine, real * sine + imag * cosine


def butterfly(values, sign):
    count = len(values)
    if count == 1:
        return values
    even = butterfly(values[0::2], sign)
    odd = butterfly(values[1::2], sign)
    low, high = [], []
    for at in range(count // 2):
        er, ei = even[at]
        tr, ti = times_unit(odd[at], at, count, sign)
        low.append((er + tr, ei + ti))
        high.append((er - tr, ei - ti))
    return low + high


def cos_sin(angle):
    half = angle * 0.5
    square = half * half
    sine = -2.5052108e-08
    for factor in (2.7557319e-06, -1.9841270e-04, 8.3333333e-03, -1.6666667e-01, 1.0):
        sine = sine * square + factor
    sine = sine * half
    cosine = 2.0876757e-09
    for factor in (-2.7557319e-07, 2.4801587e-05, -1.3888889e-03, 4.1666667e-02, -0.5, 1.0):
        cosine = cosine * square + factor
    return 1.0 - 2.0 * (sine * sine), 2.0 * (sine * cosine)


def dot(a, b):
    return jnp.dot(a, b, preferred_element_type=F32)


def dot_nt(a, b):
    return lax.dot_general(a, b, (((1,), (1,)), ((), ())), preferred_element_type=F32)


def kernel(
    shifts, mask, spec, diff, phases, trans, base_rows, base_cols, turn_rows, turn_cols,
    out,
    low0, high0, dw, trig0, trig1, wr, wc, pick_cols, pick_rows, back_rows, tspace, work,
    sa1, rb1, sb1, ra1, sd1, rd1, sd2, ra2, sa2, rb2, sb2, ra3, low1, high1,
    sa3, rb3, sb3, ra4, sd3, rd3, fs, rf, ts, tr,
    send_sem, recv_sem, halo_sem,
):
    rp = lax.axis_index("rows")
    cp = lax.axis_index("cols")

    def row_peer(step):
        return lax.rem(rp + step, NR)

    def col_peer(step):
        return lax.rem(cp + step, NC)

    barrier = pltpu.get_barrier_semaphore()
    for step in range(1, NR):
        pl.semaphore_signal(barrier, inc=1, device_id={"rows": row_peer(step)})
    for step in range(1, NC):
        pl.semaphore_signal(barrier, inc=1, device_id={"cols": col_peer(step)})
    half_row = lax.div(rp, 2)
    own_pair = half_row == cp
    for h in range(2):
        for step in range(NC):
            peer = col_peer(step)
            target = 2 * cp + h

            @pl.when(jnp.logical_or(peer != cp, target != rp))
            def _():
                pl.semaphore_signal(barrier, inc=1, device_id={"rows": target, "cols": peer})
    for step in range(NR):
        peer = row_peer(step)

        @pl.when(jnp.logical_or(peer != rp, half_row != cp))
        def _():
            pl.semaphore_signal(barrier, inc=1, device_id={"rows": peer, "cols": half_row})

    @pl.when(own_pair)
    def _():
        pl.semaphore_wait(barrier, NR - 1 + NC - 1 + 30)

    @pl.when(jnp.logical_not(own_pair))
    def _():
        pl.semaphore_wait(barrier, NR - 1 + NC - 1 + 32)

    def remote(src, dst, at, device):
        return pltpu.make_async_remote_copy(
            src_ref=src, dst_ref=dst, send_sem=send_sem.at[at], recv_sem=recv_sem.at[at], device_id=device
        )

    def rows_exchange(src, dst, at):
        for step in range(1, NR):
            peer = row_peer(step)
            remote(src.at[peer], dst.at[rp], at, {"rows": peer}).start()
        pltpu.make_async_copy(src.at[rp], dst.at[rp], recv_sem.at[at]).start()

    def cols_exchange(src, dst, at):
        for step in range(1, NC):
            peer = col_peer(step)
            remote(src.at[peer], dst.at[cp], at, {"cols": peer}).start()
        pltpu.make_async_copy(src.at[cp], dst.at[cp], recv_sem.at[at]).start()

    def arrived(dst, at):
        pltpu.make_async_copy(dst, dst, recv_sem.at[at]).wait()

    def halo_start(src, low, high, at):
        @pl.when(rp < NR - 1)
        def _():
            pltpu.make_async_remote_copy(
                src_ref=src, dst_ref=low, send_sem=halo_sem.at[at, 0], recv_sem=halo_sem.at[at, 1],
                device_id={"rows": rp + 1},
            ).start()

        @pl.when(rp > 0)
        def _():
            pltpu.make_async_remote_copy(
                src_ref=src, dst_ref=high, send_sem=halo_sem.at[at, 2], recv_sem=halo_sem.at[at, 3],
                device_id={"rows": rp - 1},
            ).start()

    def halo_wait(src, low, high, at):
        @pl.when(rp < NR - 1)
        def _():
            pltpu.make_async_copy(high, high, halo_sem.at[at, 3]).wait()
            pltpu.make_async_copy(src, src, halo_sem.at[at, 0]).wait()

        @pl.when(rp > 0)
        def _():
            pltpu.make_async_copy(low, low, halo_sem.at[at, 1]).wait()
            pltpu.make_async_copy(src, src, halo_sem.at[at, 2]).wait()

    halo_start(spec, low0, high0, 0)

    @pl.when(rp == 0)
    def _():
        low0[...] = jnp.zeros_like(low0)
        low1[...] = jnp.zeros_like(low1)

    @pl.when(rp == NR - 1)
    def _():
        high0[...] = jnp.zeros_like(high0)
        high1[...] = jnp.zeros_like(high1)

    def iota(shape, axis):
        return lax.broadcasted_iota(jnp.int32, shape, axis)

    def one_hot(test):
        return jnp.where(test, 1.0, 0.0).astype(BF16)

    lane = iota((512, 512), 1)
    pick_cols[...] = one_hot(iota((512, 512), 0) == (lane & 63) * 8 + (lane >> 6))
    a, b = iota((256, 256), 0), iota((256, 256), 1)
    pick_rows[...] = one_hot(b == (a & 15) * 16 + (a >> 4))
    back_rows[...] = one_hot(a == (b & 15) * 16 + (b >> 4))

    for half in range(2):
        cols = pl.ds(half * 256, 256)
        picked = dot(trans[...].astype(BF16), pick_cols[:, cols]).astype(BF16)
        ts[:, :, cols] = dot(pick_rows[...], picked).astype(BF16).reshape(NR, 16, 256)
    for step in range(NR):
        peer = row_peer(step)
        slot = tr.at[cp, lax.rem(rp, 2)]
        here = jnp.logical_and(peer == rp, half_row == cp)

        @pl.when(here)
        def _():
            pltpu.make_async_copy(ts.at[peer], slot, recv_sem.at[0]).start()

        @pl.when(jnp.logical_not(here))
        def _():
            remote(ts.at[peer], slot, 0, {"rows": peer, "cols": half_row}).start()

    c, s = base_rows[0], base_rows[1]
    for sign in range(2):
        t = s if sign == 0 else -s
        wr[sign, 0:256, 0:256] = c
        wr[sign, 256:512, 256:512] = c
        wr[sign, 0:256, 256:512] = t
        wr[sign, 256:512, 0:256] = -t
    c, s = base_cols[0], base_cols[1]
    for sign in range(2):
        t = s if sign == 0 else -s
        wc[sign, 0:512, 0:512] = c
        wc[sign, 512:1024, 512:1024] = c
        wc[sign, 0:512, 512:1024] = t
        wc[sign, 512:1024, 0:512] = -t

    at_j, to_j = iota((128, 256), 0), iota((128, 256), 1)
    for bounce in range(2):
        g = shifts[bounce]
        below = one_hot(to_j == at_j + 256 - g)
        above = one_hot(to_j == at_j + g - 128)
        for block in range(2):
            weights = [mask[block, m].astype(F32) for m in range(3)]
            for plane in range(2):
                left = (dot(diff[plane, block, 0], below) * weights[0]).astype(BF16)
                own = (diff[plane, block, 1].astype(F32) * weights[1]).astype(BF16)
                right = (dot(diff[plane, block, 2], above) * weights[2]).astype(BF16)
                nothing = jnp.zeros((128, 128), BF16)
                units = [left[:, :128], left[:, 128:], own, right[:, :128], right[:, 128:]]
                units = units + [nothing] if block == 0 else [nothing] + units
                for at, unit in enumerate(units):
                    which, col = at // 2, 128 * (at % 2)
                    row = 128 * block
                    if plane == 0:
                        dw[bounce, which, row:row + 128, col:col + 128] = unit
                        dw[bounce, which, 256 + row:384 + row, 256 + col:384 + col] = unit
                    else:
                        dw[bounce, which, 256 + row:384 + row, col:col + 128] = unit
                        dw[bounce, which, row:row + 128, 256 + col:384 + col] = -unit

    def phase0(at, _):
        rows = pl.ds(pl.multiple_of(at * 32, 32), 32)
        cosine, sine = cos_sin(phases[0, rows, :])
        trig0[0, rows, :] = cosine
        trig0[1, rows, :] = sine
        return 0

    lax.fori_loop(0, 8, phase0, 0)

    halo_wait(spec, low0, high0, 0)

    def diffract0(at, _):
        cols = pl.ds(pl.multiple_of(at * 128, 128), 128)
        total = None
        for which, ref in enumerate((low0, spec, high0)):
            block = ref[:, :, cols].reshape(512, 128)
            term = dot(dw[0, which], block)
            total = term if total is None else total + term
        cosine, sine = trig0[0, :, cols], trig0[1, :, cols]
        real, imag = total[:256], total[256:]
        wave_re = (real * cosine - imag * sine).astype(BF16)
        wave_im = (real * sine + imag * cosine).astype(BF16)
        sa1[pl.ds(at * 4, 4), :, 0:256] = wave_re.T.reshape(4, 32, 256)
        sa1[pl.ds(at * 4, 4), :, 256:512] = wave_im.T.reshape(4, 32, 256)
        return 0

    lax.fori_loop(0, 4, diffract0, 0)
    rows_exchange(sa1, rb1, 1)

    def phase1(at, _):
        cols = pl.ds(pl.multiple_of(at * 128, 128), 128)
        cosine, sine = cos_sin(phases[1, :, cols])
        trig1[0, cols, :] = cosine.T
        trig1[1, cols, :] = sine.T
        return 0

    lax.fori_loop(0, 4, phase1, 0)

    arrived(tr, 0)
    low_lane = iota((32, 128), 1) < 64

    def swap_halves(first, second):
        return (
            jnp.where(low_lane, first, pltpu.roll(second, 64, 1)),
            jnp.where(low_lane, pltpu.roll(first, 64, 1), second),
        )

    for e in range(4):
        for q in range(4):
            src = slice(128 * q, 128 * q + 128)
            first = tr[2 * e, :, :, src].reshape(32, 128).astype(F32)
            second = tr[2 * e + 1, :, :, src].reshape(32, 128).astype(F32)
            one, two = swap_halves(first, second)
            tspace[2 * q, :, 128 * e:128 * e + 128] = one
            tspace[2 * q + 1, :, 128 * e:128 * e + 128] = two

    def forward_rows(src, dst):
        def first(at, _):
            crow = pl.ds(pl.multiple_of(lax.div(at, 2) * 16, 16), 16)
            half = pl.multiple_of(lax.rem(at, 2) * 128, 128)
            re, im = pl.ds(half, 128), pl.ds(half + 256, 128)
            values = [(src[p, crow, re].astype(F32), src[p, crow, im].astype(F32)) for p in range(NR)]
            values = butterfly(values, 1)
            for r in range(NR):
                real, imag = values[r]
                cosine, sine = turn_rows[0, r, :, re], turn_rows[1, r, :, re]
                work[r, crow, re] = (real * cosine - imag * sine).astype(BF16)
                work[r, crow, im] = (real * sine + imag * cosine).astype(BF16)
            return 0

        lax.fori_loop(0, 4, first, 0)

        def second(at, _):
            block = pl.ds(at * 4, 4)
            got = dot(work[block].reshape(128, 512), wr[0])
            dst[block] = got.astype(BF16).reshape(4, 32, 512)
            return 0

        lax.fori_loop(0, 4, second, 0)

    def to_natural(src, dst):
        def part(at, _):
            cols = pl.ds(pl.multiple_of(at * 128, 128), 128)
            cols2 = pl.ds(pl.multiple_of(at * 128 + 512, 128), 128)
            block = src[pl.ds(at * 4, 4)].reshape(128, 512)
            dst[:, :, cols] = block[:, :256].T.reshape(8, 32, 128)
            dst[:, :, cols2] = block[:, 256:].T.reshape(8, 32, 128)
            return 0

        lax.fori_loop(0, 4, part, 0)

    def to_turned(src, dst):
        def part(at, _):
            cols = pl.ds(pl.multiple_of(at * 128, 128), 128)
            cols2 = pl.ds(pl.multiple_of(at * 128 + 512, 128), 128)
            dst[pl.ds(at * 4, 4), :, 0:256] = src[:, :, cols].reshape(256, 128).T.reshape(4, 32, 256)
            dst[pl.ds(at * 4, 4), :, 256:512] = src[:, :, cols2].reshape(256, 128).T.reshape(4, 32, 256)
            return 0

        lax.fori_loop(0, 4, part, 0)

    def forward_cols(src, dst):
        def first(at, _):
            crow = pl.ds(pl.multiple_of(lax.div(at, 4) * 16, 16), 16)
            quarter = pl.multiple_of(lax.rem(at, 4) * 128, 128)
            re, im = pl.ds(quarter, 128), pl.ds(quarter + 512, 128)
            values = [(src[p, crow, re].astype(F32), src[p, crow, im].astype(F32)) for p in range(NC)]
            values = butterfly(values, 1)
            for r in range(NC):
                real, imag = values[r]
                cosine, sine = turn_cols[0, r, :, re], turn_cols[1, r, :, re]
                dst[r, crow, re] = (real * cosine - imag * sine).astype(BF16)
                dst[r, crow, im] = (real * sine + imag * cosine).astype(BF16)
            return 0

        lax.fori_loop(0, 8, first, 0)

    def run_cols_pair(src, temp, work_f, dst):
        forward_cols(src, temp)

        def middle(at, _):
            block = pl.ds(at * 2, 2)
            space = dot(temp[block].reshape(64, 1024), wc[0])
            kept = tspace[block].reshape(64, 512)
            kept = jnp.concatenate([kept, kept], axis=1)
            back = dot((space * kept).astype(BF16), wc[1])
            work_f[block] = back.reshape(2, 32, 1024)
            return 0

        lax.fori_loop(0, 4, middle, 0)

        def last(at, _):
            crow = pl.ds(pl.multiple_of(lax.div(at, 4) * 16, 16), 16)
            quarter = pl.multiple_of(lax.rem(at, 4) * 128, 128)
            re, im = pl.ds(quarter, 128), pl.ds(quarter + 512, 128)
            values = []
            for r in range(NC):
                real, imag = work_f[r, crow, re], work_f[r, crow, im]
                cosine, sine = turn_cols[0, r, :, re], turn_cols[1, r, :, re]
                values.append((real * cosine + imag * sine, imag * cosine - real * sine))
            values = butterfly(values, -1)
            for r in range(NC):
                dst[r, crow, re] = values[r][0].astype(BF16)
                dst[r, crow, im] = values[r][1].astype(BF16)
            return 0

        lax.fori_loop(0, 8, last, 0)

    def with_scratch(temp_d, work_d, work_r):
        arrived(rb1, 1)
        forward_rows(rb1, sb1)
        rows_exchange(sb1, ra1, 2)
        arrived(ra1, 2)
        to_natural(ra1, sd1)
        cols_exchange(sd1, rd1, 3)
        arrived(rd1, 3)
        run_cols_pair(rd1, temp_d, work_d, sd2)
        cols_exchange(sd2, ra2, 4)
        arrived(ra2, 4)
        to_turned(ra2, sa2)
        rows_exchange(sa2, rb2, 5)
        arrived(rb2, 5)

        def lanes(at, _):
            block = pl.ds(at * 4, 4)
            work_r[block] = dot(rb2[block].reshape(128, 512), wr[1]).reshape(4, 32, 512)
            return 0

        lax.fori_loop(0, 4, lanes, 0)

        def sources(at, _):
            crow = pl.ds(pl.multiple_of(lax.div(at, 2) * 16, 16), 16)
            half = pl.multiple_of(lax.rem(at, 2) * 128, 128)
            re, im = pl.ds(half, 128), pl.ds(half + 256, 128)
            values = []
            for r in range(NR):
                real, imag = work_r[r, crow, re], work_r[r, crow, im]
                cosine, sine = turn_rows[0, r, :, re], turn_rows[1, r, :, re]
                values.append((real * cosine + imag * sine, imag * cosine - real * sine))
            values = butterfly(values, -1)
            for r in range(NR):
                sb2[r, crow, re] = values[r][0].astype(BF16)
                sb2[r, crow, im] = values[r][1].astype(BF16)
            return 0

        lax.fori_loop(0, 4, sources, 0)
        rows_exchange(sb2, ra3, 6)
        arrived(ra3, 6)
        halo_start(ra3, low1, high1, 1)
        halo_wait(ra3, low1, high1, 1)

        def diffract1(at, _):
            block = pl.ds(at * 4, 4)
            rows = pl.ds(pl.multiple_of(at * 128, 128), 128)
            total = None
            for which, ref in enumerate((low1, ra3, high1)):
                term = dot_nt(ref[block].reshape(128, 512), dw[1, which])
                total = term if total is None else total + term
            cosine, sine = trig1[0, rows, :], trig1[1, rows, :]
            real, imag = total[:, :256], total[:, 256:]
            sa3[block, :, 0:256] = (real * cosine - imag * sine).astype(BF16).reshape(4, 32, 256)
            sa3[block, :, 256:512] = (real * sine + imag * cosine).astype(BF16).reshape(4, 32, 256)
            return 0

        lax.fori_loop(0, 4, diffract1, 0)
        rows_exchange(sa3, rb3, 7)
        arrived(rb3, 7)
        forward_rows(rb3, sb3)
        rows_exchange(sb3, ra4, 8)
        arrived(ra4, 8)
        to_natural(ra4, sd3)
        cols_exchange(sd3, rd3, 9)
        arrived(rd3, 9)
        forward_cols(rd3, temp_d)

        def final_lanes(at, _):
            block = pl.ds(at * 2, 2)
            work_d[block] = dot(temp_d[block].reshape(64, 1024), wc[0]).reshape(2, 32, 1024)
            return 0

        lax.fori_loop(0, 4, final_lanes, 0)
        for plane in range(2):
            for q in range(4):
                for e in range(4):
                    src = slice(512 * plane + 128 * e, 512 * plane + 128 * e + 128)
                    lanes_to = slice(512 * plane + 128 * q, 512 * plane + 128 * q + 128)
                    one, two = swap_halves(work_d[2 * q, :, src], work_d[2 * q + 1, :, src])
                    fs[2 * e, :, lanes_to] = one.astype(BF16)
                    fs[2 * e + 1, :, lanes_to] = two.astype(BF16)
        for h in range(2):
            for step in range(NC):
                peer = col_peer(step)
                target = 2 * cp + h
                here = jnp.logical_and(peer == cp, target == rp)
                src = fs.at[peer, pl.ds(16 * h, 16)]

                @pl.when(here)
                def _():
                    pltpu.make_async_copy(src, rf.at[rp], recv_sem.at[10]).start()

                @pl.when(jnp.logical_not(here))
                def _():
                    remote(src, rf.at[rp], 10, {"rows": target, "cols": peer}).start()
        arrived(rf, 10)
        for plane in range(2):
            ordered = dot_nt(rf[:, :, 512 * plane:512 * plane + 512].reshape(256, 512), pick_cols[...])
            space = dot(back_rows[...], ordered.astype(BF16))
            out[plane] = space * trans[...]

    pl.run_scoped(
        with_scratch,
        pltpu.VMEM((NC, 32, 1024), BF16),
        pltpu.VMEM((NC, 32, 1024), F32),
        pltpu.VMEM((NR, 32, 512), F32),
    )

    def sent(src, at):
        pltpu.make_async_copy(src, src, send_sem.at[at]).wait()

    for at, src in ((1, sa1), (2, sb1), (5, sa2), (6, sb2), (7, sa3), (8, sb3)):
        sent(src.at[pl.ds(0, NR - 1)], at)
    for at, src in ((3, sd1), (4, sd2), (9, sd3)):
        sent(src.at[pl.ds(0, NC - 1)], at)

    @pl.when(own_pair)
    def _():
        sent(ts.at[pl.ds(0, 15)], 0)
        sent(rf.at[pl.ds(0, 15)], 10)

    @pl.when(jnp.logical_not(own_pair))
    def _():
        sent(ts, 0)
        sent(rf, 10)


def on_device(spectrum, diffraction, order_mask, phases, transmission, shifts):
    vmem = pl.BlockSpec(memory_space=pltpu.VMEM)
    smem = pl.BlockSpec(memory_space=pltpu.SMEM)
    rows_buf = pltpu.VMEM((NR, 32, 512), BF16)
    cols_buf = pltpu.VMEM((NC, 32, 1024), BF16)
    halo0 = pltpu.VMEM((2, 256, 512), BF16)
    return pl.pallas_call(
        kernel,
        out_shape=jax.ShapeDtypeStruct((2, 256, 512), F32),
        in_specs=[smem, smem] + [vmem] * 8,
        out_specs=vmem,
        scratch_shapes=[
            halo0, halo0,
            pltpu.VMEM((2, 3, 512, 512), BF16),
            pltpu.VMEM((2, 256, 512), F32),
            pltpu.VMEM((2, 512, 256), F32),
            pltpu.VMEM((2, 512, 512), BF16),
            pltpu.VMEM((2, 1024, 1024), BF16),
            pltpu.VMEM((512, 512), BF16),
            pltpu.VMEM((256, 256), BF16),
            pltpu.VMEM((256, 256), BF16),
            pltpu.VMEM((NC, 32, 512), F32),
            rows_buf,
            rows_buf, rows_buf, rows_buf, rows_buf,
            cols_buf, cols_buf, cols_buf, cols_buf,
            rows_buf, rows_buf, rows_buf, rows_buf,
            rows_buf, rows_buf,
            rows_buf, rows_buf, rows_buf, rows_buf,
            cols_buf, cols_buf, cols_buf,
            pltpu.VMEM((NR, 16, 1024), BF16),
            pltpu.VMEM((NR, 16, 512), BF16),
            pltpu.VMEM((NC, 2, 16, 512), BF16),
            pltpu.SemaphoreType.DMA((11,)),
            pltpu.SemaphoreType.DMA((11,)),
            pltpu.SemaphoreType.DMA((2, 4)),
        ],
        compiler_params=pltpu.CompilerParams(
            collective_id=0, has_side_effects=True, vmem_limit_bytes=60 * 1024 * 1024
        ),
    )(shifts, order_mask, spectrum, diffraction, phases, transmission, *tables())


def solution(mesh):
    placed = (
        P(None, "rows", "cols"),
        P(None, "rows", None, None, None),
        P("rows", None),
        P(None, "rows", "cols"),
        P("rows", "cols"),
        P(),
    )
    return jax.shard_map(
        on_device, mesh=mesh, in_specs=placed, out_specs=P(None, "rows", "cols"), check_vma=False
    )
```

time: 635 us -> 149 us (0.23)
  the two profiles are of different devices: /device:TPU:1 before, /device:TPU:57 now
where the time goes in v1:
time: 149 us
  Pallas kernels  146 us (98%)
  local copies, waits for them, and re-layouts  2.26 us (2%)
    pallas_call x1, Pallas kernels, on_device(): pl.pallas_call(kernel, out_shape=jax.ShapeDtypeStruct((2, 256, 512), F32)...  146 us

profile of v1, /device:TPU:57, one launch (start us, length us, event | category | flops | bytes accessed | tf_op | source)
XLA Modules:
  0.0 148.7 jit_solution(10594963002691807992)
XLA Ops:
  0.0 146.5 %shard_map.100 = f32[2,256,512]{2,1,0:T(8,128)} custom-call(s32[2]{0:T(128)} %shifts.1, s32[2,3]{1,0:T(2,128)} %mask.1, bf16[2,256,512]{2,1,0:T(8,128)(2,1)} %spec.1, bf16[2,2,3,128,128]{4,3,2,1,0:T(8,128)(2,1)} %diff.1, f32[2,256,512]{2,1,0:T(8,128)} %phases.1, f32[256,512]{1,0:T(8,128)} %trans.1, bf16[2,256,256]{2,1,0:T(8,128)(2,1)} %constant.8.clone.base_rows, ...), custom_call_target="tpu_custom_call" | custom-call | tf_op jit(solution)/shard_map/pallas_call | solution.py:552
  146.5 2.3 %copy.12 = f32[2,256,512]{2,1,0:T(8,128)} copy(f32[2,256,512]{2,1,0:T(8,128)} %shard_map.100) | data formatting | bytes 2097152

commit v2 on v0

v2 whole, which is shorter than its diff:
```python
import math

import jax
import jax.numpy as jnp
import numpy as np
from jax import lax
from jax.experimental import pallas as pl
from jax.experimental.pallas import tpu as pltpu
from jax.sharding import PartitionSpec as P

F32 = jnp.float32
BF16 = jnp.bfloat16
NR = 16
NC = 8
FULL = 4096


def tables():
    def circle(count, left, right):
        angle = 2.0 * np.pi * ((left[:, None] * right[None, :]) % count) / count
        return np.cos(angle), np.sin(angle)

    at = np.arange(512)
    row = 32 * (at // 16 % 8) + 8 * (at // 128) + at % 8
    imaginary = at // 8 % 2 == 1
    c, s = circle(256, np.arange(256), row)
    base_rows = np.concatenate([np.where(imaginary, s, c), np.where(imaginary, c, -s)]) / 64.0
    at = np.arange(512)
    col = 256 * (at // 16 % 2) + 16 * (at // 32) + at % 16
    base_cols = np.stack(circle(512, col, np.arange(512))) / 64.0
    turn_rows = np.stack(circle(FULL, np.arange(NR), np.arange(256)))[:, :, None, :]
    turn_cols = np.stack(circle(FULL, np.arange(NC), col))
    by_source = turn_cols.reshape(2, NC, NR, 1, 32)
    by_source = np.tile(by_source, (1, 1, 1, 1, 4))
    by_lane = turn_cols.reshape(2, NC, 4, 1, 128)
    return (
        jnp.asarray(base_rows, BF16),
        jnp.asarray(base_cols, BF16),
        jnp.asarray(turn_rows, F32),
        jnp.asarray(by_source, F32),
        jnp.asarray(by_lane, F32),
    )


def times_unit(value, numerator, count, sign):
    real, imag = value
    step = (numerator * 8) % (count * 8)
    eighth, rest = divmod(step, count)
    if rest == 0 and eighth % 2 == 0:
        quarter = (eighth // 2) % 4
        if quarter == 0:
            return real, imag
        if quarter == 2:
            return -real, -imag
        if (quarter == 1) == (sign > 0):
            return -imag, real
        return imag, -real
    angle = 2.0 * math.pi * numerator / count
    cosine, sine = math.cos(angle), sign * math.sin(angle)
    if rest == 0:
        half = abs(cosine)
        a = (real - imag) if cosine * sine > 0 else (real + imag)
        b = (real + imag) if cosine * sine > 0 else (imag - real)
        if cosine < 0:
            return a * (-half), b * (-half)
        return a * half, b * half
    return real * cosine - imag * sine, real * sine + imag * cosine


def butterfly(values, sign):
    count = len(values)
    if count == 1:
        return values
    even = butterfly(values[0::2], sign)
    odd = butterfly(values[1::2], sign)
    low, high = [], []
    for at in range(count // 2):
        er, ei = even[at]
        tr, ti = times_unit(odd[at], at, count, sign)
        low.append((er + tr, ei + ti))
        high.append((er - tr, ei - ti))
    return low + high


def cos_sin(angle):
    half = angle * 0.5
    square = half * half
    sine = -2.5052108e-08
    for factor in (2.7557319e-06, -1.9841270e-04, 8.3333333e-03, -1.6666667e-01, 1.0):
        sine = sine * square + factor
    sine = sine * half
    cosine = 2.0876757e-09
    for factor in (-2.7557319e-07, 2.4801587e-05, -1.3888889e-03, 4.1666667e-02, -0.5, 1.0):
        cosine = cosine * square + factor
    return 1.0 - 2.0 * (sine * sine), 2.0 * (sine * cosine)


def dot(a, b):
    return jnp.dot(a, b, preferred_element_type=F32)


def dot_nt(a, b):
    return lax.dot_general(a, b, (((1,), (1,)), ((), ())), preferred_element_type=F32)


def kernel(
    shifts, mask, spec_h, diff_h, phases_h, trans_h, base_rows_h, base_cols_h, turn_rows_h, turn_source_h,
    turn_lane_h, out_h,
    spec, diff, phases, trans, wr, base_cols, turn_rows, turn_source, turn_lane, out,
    low0, high0, dw, trig0, trig1, wc, pick_cols, pick_rows, back_rows, tspace,
    work_b, work_z, work_r, work_d, work_s, work_f,
    sa1, rb1, sm1, rd1, sm2, rb2, sb2, ra3, low1, high1, sa3, rb3, sm3, rd3, fs, rf, ts, tr,
    in_sem, send_sem, recv_sem, halo_sem, ready_sem,
):
    rp = lax.axis_index("rows")
    cp = lax.axis_index("cols")

    def row_peer(step):
        return lax.rem(rp + step, NR)

    def col_peer(step):
        return lax.rem(cp + step, NC)

    barrier = pltpu.get_barrier_semaphore()
    for step in range(1, NR):
        pl.semaphore_signal(barrier, inc=1, device_id={"rows": row_peer(step)})
    for step in range(1, NC):
        pl.semaphore_signal(barrier, inc=1, device_id={"cols": col_peer(step)})

    loads = {}
    for at, (name, src, dst) in enumerate((
        ("diff", diff_h, diff), ("phases", phases_h, phases), ("spec", spec_h, spec),
        ("wr", base_rows_h, wr), ("turn_rows", turn_rows_h, turn_rows), ("trans", trans_h, trans),
        ("base_cols", base_cols_h, base_cols), ("turn_source", turn_source_h, turn_source),
        ("turn_lane", turn_lane_h, turn_lane),
    )):
        loads[name] = pltpu.make_async_copy(src, dst, in_sem.at[at])
        loads[name].start()

    def remote(src, dst, at, device):
        return pltpu.make_async_remote_copy(
            src_ref=src, dst_ref=dst, send_sem=send_sem.at[at], recv_sem=recv_sem.at[at], device_id=device
        )

    def rows_exchange(src, dst, at):
        for step in range(1, NR):
            peer = row_peer(step)
            remote(src.at[peer], dst.at[rp], at, {"rows": peer}).start()
        pltpu.make_async_copy(src.at[rp], dst.at[rp], recv_sem.at[at]).start()

    def arrived(dst, at):
        pltpu.make_async_copy(dst, dst, recv_sem.at[at]).wait()

    def sent(src, at):
        pltpu.make_async_copy(src, src, send_sem.at[at]).wait()

    def halo_start(src, low, high, at):
        @pl.when(rp < NR - 1)
        def _():
            pltpu.make_async_remote_copy(
                src_ref=src, dst_ref=low, send_sem=halo_sem.at[at, 0], recv_sem=halo_sem.at[at, 1],
                device_id={"rows": rp + 1},
            ).start()

        @pl.when(rp > 0)
        def _():
            pltpu.make_async_remote_copy(
                src_ref=src, dst_ref=high, send_sem=halo_sem.at[at, 2], recv_sem=halo_sem.at[at, 3],
                device_id={"rows": rp - 1},
            ).start()

    def halo_wait(low, high, at):
        @pl.when(rp < NR - 1)
        def _():
            pltpu.make_async_copy(high, high, halo_sem.at[at, 3]).wait()

        @pl.when(rp > 0)
        def _():
            pltpu.make_async_copy(low, low, halo_sem.at[at, 1]).wait()

    def halo_sent(src, at):
        @pl.when(rp < NR - 1)
        def _():
            pltpu.make_async_copy(src, src, halo_sem.at[at, 0]).wait()

        @pl.when(rp > 0)
        def _():
            pltpu.make_async_copy(src, src, halo_sem.at[at, 2]).wait()

    def iota(shape, axis):
        return lax.broadcasted_iota(jnp.int32, shape, axis)

    def one_hot(test):
        return jnp.where(test, 1.0, 0.0).astype(BF16)

    at_j, to_j = iota((128, 256), 0), iota((128, 256), 1)

    def banded(bounce):
        g = shifts[bounce]
        below = one_hot(to_j == at_j + 256 - g)
        above = one_hot(to_j == at_j + g - 128)
        for block in range(2):
            weights = [mask[block, m].astype(F32) for m in range(3)]
            for plane in range(2):
                left = (dot(diff[plane, block, 0], below) * weights[0]).astype(BF16)
                own = (diff[plane, block, 1].astype(F32) * weights[1]).astype(BF16)
                right = (dot(diff[plane, block, 2], above) * weights[2]).astype(BF16)
                nothing = jnp.zeros((128, 128), BF16)
                units = [left[:, :128], left[:, 128:], own, right[:, :128], right[:, 128:]]
                units = units + [nothing] if block == 0 else [nothing] + units
                for at, unit in enumerate(units):
                    which, col = at // 2, 128 * (at % 2)
                    row = 128 * block
                    if plane == 0:
                        dw[bounce, which, row:row + 128, col:col + 128] = unit
                        dw[bounce, which, 256 + row:384 + row, 256 + col:384 + col] = unit
                    else:
                        dw[bounce, which, 256 + row:384 + row, col:col + 128] = unit
                        dw[bounce, which, row:row + 128, 256 + col:384 + col] = -unit

    loads["diff"].wait()
    banded(0)

    @pl.when(rp == 0)
    def _():
        low0[...] = jnp.zeros_like(low0)
        low1[...] = jnp.zeros_like(low1)

    @pl.when(rp == NR - 1)
    def _():
        high0[...] = jnp.zeros_like(high0)
        high1[...] = jnp.zeros_like(high1)

    pl.semaphore_wait(barrier, NR - 1 + NC - 1)
    for h in range(2):
        halo_start(spec_h.at[:, :, pl.ds(256 * h, 256)], low0.at[h], high0.at[h], h)
    for step in range(1, NC):
        pl.semaphore_signal(ready_sem, inc=1, device_id={"cols": col_peer(step)})

    loads["phases"].wait()

    def phase0(at, _):
        rows = pl.ds(pl.multiple_of(at * 32, 32), 32)
        cosine, sine = cos_sin(phases[0, rows, :])
        trig0[0, rows, :] = cosine
        trig0[1, rows, :] = sine
        return 0

    lax.fori_loop(0, 8, phase0, 0)
    loads["spec"].wait()

    for h in range(2):
        halo_wait(low0.at[h], high0.at[h], h)
        for part in range(2):
            cols = slice(256 * h + 128 * part, 256 * h + 128 * part + 128)
            here = slice(128 * part, 128 * part + 128)
            total = dot(dw[0, 1], spec[:, :, cols].reshape(512, 128))
            total = total + dot(dw[0, 0], low0[h, :, :, here].reshape(512, 128))
            total = total + dot(dw[0, 2], high0[h, :, :, here].reshape(512, 128))
            cosine, sine = trig0[0, :, cols], trig0[1, :, cols]
            real, imag = total[:256], total[256:]
            wave_re = (real * cosine - imag * sine).astype(BF16)
            wave_im = (real * sine + imag * cosine).astype(BF16)
            sa1[h, 8 * part:8 * part + 8, :, 0:256] = wave_re.T.reshape(8, 16, 256)
            sa1[h, 8 * part:8 * part + 8, :, 256:512] = wave_im.T.reshape(8, 16, 256)
        rows_exchange(sa1.at[h], rb1.at[h], 1 + h)

    pl.semaphore_wait(ready_sem, NC - 1)

    lane = iota((512, 512), 1)
    pick_cols[...] = one_hot(iota((512, 512), 0) == (lane & 63) * 8 + (lane >> 6))
    a, b = iota((256, 256), 0), iota((256, 256), 1)
    pick_rows[...] = one_hot(b == (a & 15) * 16 + (a >> 4))
    back_rows[...] = one_hot(a == (b & 15) * 16 + (b >> 4))

    half_row = lax.div(rp, 2)
    own_pair = half_row == cp
    loads["trans"].wait()
    for half in range(2):
        cols = pl.ds(half * 256, 256)
        picked = dot(trans[...].astype(BF16), pick_cols[:, cols]).astype(BF16)
        ts[:, :, cols] = dot(pick_rows[...], picked).astype(BF16).reshape(NR, 16, 256)
    for step in range(NR):
        peer = row_peer(step)
        slot = tr.at[cp, lax.rem(rp, 2)]
        here = jnp.logical_and(peer == rp, own_pair)

        @pl.when(here)
        def _():
            pltpu.make_async_copy(ts.at[peer], slot, recv_sem.at[0]).start()

        @pl.when(jnp.logical_not(here))
        def _():
            remote(ts.at[peer], slot, 0, {"rows": peer, "cols": half_row}).start()

    loads["base_cols"].wait()
    c, s = base_cols[0], base_cols[1]
    wc[0:512, 0:512] = c
    wc[512:1024, 512:1024] = c
    wc[0:512, 512:1024] = s
    wc[512:1024, 0:512] = -s
    for name in ("wr", "turn_rows", "turn_source", "turn_lane"):
        loads[name].wait()

    lane128 = iota((1, 128), 1)
    low_half = lane128 < 64
    even_group = (lane128 & 32) == 0

    def swap_halves(first, second):
        return (
            jnp.where(low_half, first, pltpu.roll(second, 64, 1)),
            jnp.where(low_half, pltpu.roll(first, 64, 1), second),
        )

    def swap_groups(first, second):
        return (
            jnp.where(even_group, first, pltpu.roll(second, 32, 1)),
            jnp.where(even_group, pltpu.roll(first, 96, 1), second),
        )

    def quad(values):
        p0, p2 = swap_halves(values[0], values[2])
        p1, p3 = swap_halves(values[1], values[3])
        b0, b1 = swap_groups(p0, p1)
        b2, b3 = swap_groups(p2, p3)
        return [b0, b1, b2, b3]

    def forward_rows(src, h):
        def first(at, _):
            half = pl.multiple_of(at * 128, 128)
            re, im = pl.ds(half, 128), pl.ds(half + 256, 128)
            values = [(src[p, :, re].astype(F32), src[p, :, im].astype(F32)) for p in range(NR)]
            values = butterfly(values, 1)
            for r in range(NR):
                real, imag = values[r]
                cosine, sine = turn_rows[0, r, :, re], turn_rows[1, r, :, re]
                work_b[r, :, re] = (real * cosine - imag * sine).astype(BF16)
                work_b[r, :, im] = (real * sine + imag * cosine).astype(BF16)
            return 0

        lax.fori_loop(0, 2, first, 0)
        for part in range(2):
            lanes = slice(256 * part, 256 * part + 256)
            got = dot(work_b[...].reshape(256, 512), wr[:, lanes])
            work_z[:, 16 * h:16 * h + 16, lanes] = got.astype(BF16).reshape(NR, 16, 256)

    def mesh_send(src, dst, slot, at, r, g):
        remote(src.at[r, g], dst.at[slot], at, {"rows": r, "cols": g}).start()

    def to_cols(send, recv, at):
        def turn(step):
            r = row_peer(step)
            block = work_z[r]
            block = jnp.concatenate([block[:, 128 * u:128 * u + 128] for u in range(4)], axis=0)
            send[r] = block.T.reshape(NC, 16, 128)
            return r

        def others(step, _):
            r = turn(step)
            for away in range(NC):
                g = col_peer(away)
                remote(send.at[r, g], recv.at[cp, rp], at, {"rows": r, "cols": g}).start()
            return 0

        lax.fori_loop(1, NR, others, 0)
        turn(0)
        for away in range(1, NC):
            g = col_peer(away)
            remote(send.at[rp, g], recv.at[cp, rp], at, {"rows": rp, "cols": g}).start()
        pltpu.make_async_copy(send.at[rp, cp], recv.at[cp, rp], recv_sem.at[at]).start()

    def forward_cols(src):
        def first(at, _):
            turned = []
            for low in range(4):
                t = at * 4 + low
                values = []
                for p in range(NC):
                    tile = src[p, t].astype(F32)
                    values.append((tile[:8], tile[8:]))
                values = butterfly(values, 1)
                for r in range(NC):
                    real, imag = values[r]
                    cosine, sine = turn_source[0, r, t], turn_source[1, r, t]
                    values[r] = (real * cosine - imag * sine, real * sine + imag * cosine)
                turned.append(values)
            for r in range(NC):
                for plane in range(2):
                    lanes = pl.ds(pl.multiple_of(at * 128 + 512 * plane, 128), 128)
                    rows = quad([turned[low][r][plane] for low in range(4)])
                    work_d[r, :, lanes] = jnp.concatenate(rows, axis=0).astype(BF16)
            return 0

        lax.fori_loop(0, 4, first, 0)

    def phase1(at, _):
        cols = pl.ds(pl.multiple_of(at * 128, 128), 128)
        cosine, sine = cos_sin(phases[1, :, cols])
        trig1[0, cols, :] = cosine.T
        trig1[1, cols, :] = sine.T
        return 0

    for h in range(2):
        arrived(rb1.at[h], 1 + h)
        forward_rows(rb1.at[h], h)
    to_cols(sm1, rd1, 3)

    lax.fori_loop(0, 4, phase1, 0)
    banded(1)

    arrived(tr, 0)
    for e in range(4):
        for q in range(4):
            src = slice(128 * q, 128 * q + 128)
            first = tr[2 * e, :, :, src].reshape(32, 128).astype(F32)
            second = tr[2 * e + 1, :, :, src].reshape(32, 128).astype(F32)
            one, two = swap_halves(first, second)
            tspace[2 * q, :, 128 * e:128 * e + 128] = one
            tspace[2 * q + 1, :, 128 * e:128 * e + 128] = two

    arrived(rd1, 3)
    forward_cols(rd1)
    for part in range(4):
        lanes = slice(256 * part, 256 * part + 256)
        kept = slice(256 * (part % 2), 256 * (part % 2) + 256)
        space = dot(work_d[...].reshape(256, 1024), wc[:, lanes])
        work_s[:, lanes] = (space * tspace[:, :, kept].reshape(256, 256)).astype(BF16)
    for part in range(4):
        lanes = slice(256 * part, 256 * part + 256)
        work_f[:, :, lanes] = dot_nt(work_s[...], wc[lanes, :]).reshape(NC, 32, 256)

    def last_cols(at, _):
        re = pl.ds(pl.multiple_of(at * 128, 128), 128)
        im = pl.ds(pl.multiple_of(at * 128 + 512, 128), 128)
        parts = []
        for u in range(4):
            values = []
            for r in range(NC):
                real, imag = work_f[r, 8 * u:8 * u + 8, re], work_f[r, 8 * u:8 * u + 8, im]
                cosine, sine = turn_lane[0, r, at], turn_lane[1, r, at]
                values.append((real * cosine + imag * sine, imag * cosine - real * sine))
            parts.append(butterfly(values, -1))
        for q in range(NC):
            reals = quad([parts[u][q][0] for u in range(4)])
            imags = quad([parts[u][q][1] for u in range(4)])
            for low in range(4):
                sm2[at * 4 + low, q] = jnp.concatenate([reals[low], imags[low]], axis=0).astype(BF16)
        return 0

    lax.fori_loop(0, 4, last_cols, 0)

    def send_back(step, _):
        t = row_peer(step)
        for away in range(NC):
            g = col_peer(away)
            remote(sm2.at[t, g], rb2.at[rp, cp], 4, {"rows": t, "cols": g}).start()
        return 0

    lax.fori_loop(1, NR, send_back, 0)
    for away in range(1, NC):
        g = col_peer(away)
        remote(sm2.at[rp, g], rb2.at[rp, cp], 4, {"rows": rp, "cols": g}).start()
    pltpu.make_async_copy(sm2.at[rp, cp], rb2.at[rp, cp], recv_sem.at[4]).start()
    arrived(rb2, 4)

    def untile(s, _):
        block = rb2[s].reshape(128, 128).T
        for u in range(4):
            work_z[s, :, 128 * u:128 * u + 128] = block[32 * u:32 * u + 32]
        return 0

    lax.fori_loop(0, NR, untile, 0)
    for h in range(2):
        for part in range(2):
            lanes = slice(256 * part, 256 * part + 256)
            rows = work_z[:, 16 * h:16 * h + 16, :].reshape(256, 512)
            work_r[:, :, lanes] = dot_nt(rows, wr[lanes, :]).reshape(NR, 16, 256)

        def sources(at, _):
            half = pl.multiple_of(at * 128, 128)
            re, im = pl.ds(half, 128), pl.ds(half + 256, 128)
            values = []
            for r in range(NR):
                real, imag = work_r[r, :, re], work_r[r, :, im]
                cosine, sine = turn_rows[0, r, :, re], turn_rows[1, r, :, re]
                values.append((real * cosine + imag * sine, imag * cosine - real * sine))
            values = butterfly(values, -1)
            for r in range(NR):
                sb2[h, r, :, re] = values[r][0].astype(BF16)
                sb2[h, r, :, im] = values[r][1].astype(BF16)
            return 0

        lax.fori_loop(0, 2, sources, 0)
        rows_exchange(sb2.at[h], ra3.at[h], 5 + h)

    for h in range(2):
        arrived(ra3.at[h], 5 + h)
        halo_start(ra3.at[h], low1.at[h], high1.at[h], 2 + h)

    for h in range(2):
        halo_wait(low1.at[h], high1.at[h], 2 + h)
        total = dot_nt(ra3[h].reshape(256, 512), dw[1, 1])
        total = total + dot_nt(low1[h].reshape(256, 512), dw[1, 0])
        total = total + dot_nt(high1[h].reshape(256, 512), dw[1, 2])
        rows = slice(256 * h, 256 * h + 256)
        cosine, sine = trig1[0, rows, :], trig1[1, rows, :]
        real, imag = total[:, :256], total[:, 256:]
        sa3[h, :, :, 0:256] = (real * cosine - imag * sine).astype(BF16).reshape(NR, 16, 256)
        sa3[h, :, :, 256:512] = (real * sine + imag * cosine).astype(BF16).reshape(NR, 16, 256)
        rows_exchange(sa3.at[h], rb3.at[h], 7 + h)
    for h in range(2):
        arrived(rb3.at[h], 7 + h)
        forward_rows(rb3.at[h], h)
    to_cols(sm3, rd3, 9)
    arrived(rd3, 9)
    forward_cols(rd3)
    for part in range(4):
        lanes = slice(256 * part, 256 * part + 256)
        work_f[:, :, lanes] = dot(work_d[...].reshape(256, 1024), wc[:, lanes]).reshape(NC, 32, 256)
    for plane in range(2):
        for q in range(4):
            for e in range(4):
                src = slice(512 * plane + 128 * e, 512 * plane + 128 * e + 128)
                lanes_to = slice(512 * plane + 128 * q, 512 * plane + 128 * q + 128)
                one, two = swap_halves(work_f[2 * q, :, src], work_f[2 * q + 1, :, src])
                fs[2 * e, :, lanes_to] = one.astype(BF16)
                fs[2 * e + 1, :, lanes_to] = two.astype(BF16)
    for h in range(2):
        for step in range(NC):
            peer = col_peer(step)
            target = 2 * cp + h
            here = jnp.logical_and(peer == cp, target == rp)
            src = fs.at[peer, pl.ds(16 * h, 16)]

            @pl.when(here)
            def _():
                pltpu.make_async_copy(src, rf.at[rp], recv_sem.at[10]).start()

            @pl.when(jnp.logical_not(here))
            def _():
                remote(src, rf.at[rp], 10, {"rows": target, "cols": peer}).start()
    arrived(rf, 10)
    for plane in range(2):
        ordered = dot_nt(rf[:, :, 512 * plane:512 * plane + 512].reshape(256, 512), pick_cols[...])
        space = dot(back_rows[...], ordered.astype(BF16))
        out[plane] = space * trans[...]
        pltpu.make_async_copy(out.at[plane], out_h.at[plane], in_sem.at[9 + plane]).start()

    for h in range(2):
        halo_sent(spec_h.at[:, :, pl.ds(256 * h, 256)], h)
        halo_sent(ra3.at[h], 2 + h)
        for at, src in ((1, sa1), (5, sb2), (7, sa3)):
            sent(src.at[h, pl.ds(0, NR - 1)], at + h)
    for at, src in ((3, sm1), (4, sm2), (9, sm3)):
        sent(src.at[pl.ds(0, NR - 1)], at)
        sent(src.at[0, pl.ds(0, NC - 1)], at)

    @pl.when(own_pair)
    def _():
        sent(ts.at[pl.ds(0, 15)], 0)
        sent(rf.at[pl.ds(0, 15)], 10)

    @pl.when(jnp.logical_not(own_pair))
    def _():
        sent(ts, 0)
        sent(rf, 10)

    for plane in range(2):
        pltpu.make_async_copy(out.at[plane], out_h.at[plane], in_sem.at[9 + plane]).wait()


def on_device(spectrum, diffraction, order_mask, phases, transmission, shifts):
    anywhere = pl.BlockSpec(memory_space=pl.ANY)
    smem = pl.BlockSpec(memory_space=pltpu.SMEM)
    constants = tables()
    operands = (spectrum, diffraction, phases, transmission) + constants

    def vmem(kind, *shape):
        return pltpu.VMEM(shape, kind)

    halves = (2, NR, 16, 512)
    return pl.pallas_call(
        kernel,
        out_shape=jax.ShapeDtypeStruct((2, 256, 512), F32),
        in_specs=[smem, smem] + [anywhere] * len(operands),
        out_specs=anywhere,
        scratch_shapes=[pltpu.VMEM(x.shape, x.dtype) for x in operands] + [
            vmem(F32, 2, 256, 512),
            vmem(BF16, 2, 2, 256, 256), vmem(BF16, 2, 2, 256, 256),
            vmem(BF16, 2, 3, 512, 512),
            vmem(F32, 2, 256, 512),
            vmem(F32, 2, 512, 256),
            vmem(BF16, 1024, 1024),
            vmem(BF16, 512, 512), vmem(BF16, 256, 256), vmem(BF16, 256, 256),
            vmem(F32, NC, 32, 512),
            vmem(BF16, NR, 16, 512),
            vmem(BF16, NR, 32, 512),
            vmem(F32, NR, 16, 512),
            vmem(BF16, NC, 32, 1024),
            vmem(BF16, 256, 1024),
            vmem(F32, NC, 32, 1024),
            vmem(BF16, *halves), vmem(BF16, *halves),
            vmem(BF16, NR, NC, 16, 128), vmem(BF16, NC, NR, 16, 128),
            vmem(BF16, NR, NC, 16, 128), vmem(BF16, NR, NC, 16, 128),
            vmem(BF16, *halves), vmem(BF16, *halves),
            vmem(BF16, *halves), vmem(BF16, *halves),
            vmem(BF16, *halves), vmem(BF16, *halves),
            vmem(BF16, NR, NC, 16, 128), vmem(BF16, NC, NR, 16, 128),
            vmem(BF16, NC, 32, 1024), vmem(BF16, NR, 16, 1024),
            vmem(BF16, NR, 16, 512), vmem(BF16, NC, 2, 16, 512),
            pltpu.SemaphoreType.DMA((11,)),
            pltpu.SemaphoreType.DMA((11,)),
            pltpu.SemaphoreType.DMA((11,)),
            pltpu.SemaphoreType.DMA((4, 4)),
            pltpu.SemaphoreType.REGULAR,
        ],
        compiler_params=pltpu.CompilerParams(
            collective_id=0, has_side_effects=True, vmem_limit_bytes=60 * 1024 * 1024
        ),
    )(shifts, order_mask, *operands)


def solution(mesh):
    placed = (
        P(None, "rows", "cols"),
        P(None, "rows", None, None, None),
        P("rows", None),
        P(None, "rows", "cols"),
        P("rows", "cols"),
        P(),
    )
    return jax.shard_map(
        on_device, mesh=mesh, in_specs=placed, out_specs=P(None, "rows", "cols"), check_vma=False
    )
```

time: 635 us -> 115 us (0.18)
  the two profiles are of different devices: /device:TPU:1 before, /device:TPU:49 now
where the time goes in v2:
time: 115 us
  Pallas kernels  113 us (98%)
  local copies, waits for them, and re-layouts  2.26 us (2%)
    pallas_call x1, Pallas kernels, on_device(): pl.pallas_call(kernel, out_shape=jax.ShapeDtypeStruct((2, 256, 512), F32)...  113 us

profile of v2, /device:TPU:49, one launch (start us, length us, event | category | flops | bytes accessed | tf_op | source)
XLA Modules:
  0.0 114.8 jit_solution(7639819948691432845)
XLA Ops:
  0.0 112.6 %shard_map.109 = f32[2,256,512]{2,1,0:T(8,128)} custom-call(s32[2]{0:T(128)} %shifts.1, s32[2,3]{1,0:T(2,128)} %mask.1, bf16[2,256,512]{2,1,0:T(8,128)(2,1)} %spec_h.1, bf16[2,2,3,128,128]{4,3,2,1,0:T(8,128)(2,1)} %diff_h.1, f32[2,256,512]{2,1,0:T(8,128)} %phases_h.1, f32[256,512]{1,0:T(8,128)} %trans_h.1, bf16[512,512]{1,0:T(8,128)(2,1)} %constant.10.clone.base_rows_h, ...), custom_call_target="tpu_custom_call" | custom-call | tf_op jit(solution)/shard_map/pallas_call | solution.py:582
  112.6 2.3 %copy.13 = f32[2,256,512]{2,1,0:T(8,128)} copy(f32[2,256,512]{2,1,0:T(8,128)} %shard_map.109) | data formatting | bytes 2097152

commit v3 on v2

--- a/solution.py
+++ b/solution.py
@@ -21,24 +21,19 @@
         return np.cos(angle), np.sin(angle)
 
     at = np.arange(512)
-    row = 32 * (at // 16 % 8) + 8 * (at // 128) + at % 8
-    imaginary = at // 8 % 2 == 1
+    row = 16 * (at // 8 % 16) + 8 * (at // 256) + at % 8
+    imaginary = at // 128 % 2 == 1
     c, s = circle(256, np.arange(256), row)
     base_rows = np.concatenate([np.where(imaginary, s, c), np.where(imaginary, c, -s)]) / 64.0
-    at = np.arange(512)
     col = 256 * (at // 16 % 2) + 16 * (at // 32) + at % 16
     base_cols = np.stack(circle(512, col, np.arange(512))) / 64.0
     turn_rows = np.stack(circle(FULL, np.arange(NR), np.arange(256)))[:, :, None, :]
-    turn_cols = np.stack(circle(FULL, np.arange(NC), col))
-    by_source = turn_cols.reshape(2, NC, NR, 1, 32)
-    by_source = np.tile(by_source, (1, 1, 1, 1, 4))
-    by_lane = turn_cols.reshape(2, NC, 4, 1, 128)
+    turn_cols = np.stack(circle(FULL, np.arange(NC), col)).reshape(2, NC, 4, 1, 128)
     return (
         jnp.asarray(base_rows, BF16),
         jnp.asarray(base_cols, BF16),
         jnp.asarray(turn_rows, F32),
-        jnp.asarray(by_source, F32),
-        jnp.asarray(by_lane, F32),
+        jnp.asarray(turn_cols, F32),
     )
 
 
@@ -104,11 +99,10 @@
 
 
 def kernel(
-    shifts, mask, spec_h, diff_h, phases_h, trans_h, base_rows_h, base_cols_h, turn_rows_h, turn_source_h,
-    turn_lane_h, out_h,
-    spec, diff, phases, trans, wr, base_cols, turn_rows, turn_source, turn_lane, out,
+    shifts, mask, spec_h, diff_h, phases_h, trans_h, base_rows_h, base_cols_h, turn_rows_h, turn_cols_h, out_h,
+    spec, diff, phases, trans, wr, base_cols, turn_rows, turn_cols, out,
     low0, high0, dw, trig0, trig1, wc, pick_cols, pick_rows, back_rows, tspace,
-    work_b, work_z, work_r, work_d, work_s, work_f,
+    work_b, work_z, work_y, work_r, work_d, work_s, work_f, work_o,
     sa1, rb1, sm1, rd1, sm2, rb2, sb2, ra3, low1, high1, sa3, rb3, sm3, rd3, fs, rf, ts, tr,
     in_sem, send_sem, recv_sem, halo_sem, ready_sem,
 ):
@@ -121,6 +115,12 @@
     def col_peer(step):
         return lax.rem(cp + step, NC)
 
+    waits = []
+
+    def finish():
+        for wait in waits:
+            wait()
+
     barrier = pltpu.get_barrier_semaphore()
     for step in range(1, NR):
         pl.semaphore_signal(barrier, inc=1, device_id={"rows": row_peer(step)})
@@ -131,8 +131,7 @@
     for at, (name, src, dst) in enumerate((
         ("diff", diff_h, diff), ("phases", phases_h, phases), ("spec", spec_h, spec),
         ("wr", base_rows_h, wr), ("turn_rows", turn_rows_h, turn_rows), ("trans", trans_h, trans),
-        ("base_cols", base_cols_h, base_cols), ("turn_source", turn_source_h, turn_source),
-        ("turn_lane", turn_lane_h, turn_lane),
+        ("base_cols", base_cols_h, base_cols), ("turn_cols", turn_cols_h, turn_cols),
     )):
         loads[name] = pltpu.make_async_copy(src, dst, in_sem.at[at])
         loads[name].start()
@@ -147,6 +146,14 @@
             peer = row_peer(step)
             remote(src.at[peer], dst.at[rp], at, {"rows": peer}).start()
         pltpu.make_async_copy(src.at[rp], dst.at[rp], recv_sem.at[at]).start()
+        waits.append(lambda: sent(src.at[pl.ds(0, NR - 1)], at))
+
+    def cols_exchange(src, dst, at):
+        for step in range(1, NC):
+            peer = col_peer(step)
+            remote(src.at[peer], dst.at[cp], at, {"cols": peer}).start()
+        pltpu.make_async_copy(src.at[cp], dst.at[cp], recv_sem.at[at]).start()
+        waits.append(lambda: sent(src.at[pl.ds(0, NC - 1)], at))
 
     def arrived(dst, at):
         pltpu.make_async_copy(dst, dst, recv_sem.at[at]).wait()
@@ -168,6 +175,8 @@
                 src_ref=src, dst_ref=high, send_sem=halo_sem.at[at, 2], recv_sem=halo_sem.at[at, 3],
                 device_id={"rows": rp - 1},
             ).start()
+
+        waits.append(lambda: halo_sent(src, at))
 
     def halo_wait(low, high, at):
         @pl.when(rp < NR - 1)
@@ -271,27 +280,14 @@
     pick_cols[...] = one_hot(iota((512, 512), 0) == (lane & 63) * 8 + (lane >> 6))
     a, b = iota((256, 256), 0), iota((256, 256), 1)
     pick_rows[...] = one_hot(b == (a & 15) * 16 + (a >> 4))
-    back_rows[...] = one_hot(a == (b & 15) * 16 + (b >> 4))
-
-    half_row = lax.div(rp, 2)
-    own_pair = half_row == cp
+    back_rows[...] = one_hot(b == (a & 1) * 128 + ((a & 15) >> 1) * 16 + (a >> 4))
+
     loads["trans"].wait()
     for half in range(2):
         cols = pl.ds(half * 256, 256)
         picked = dot(trans[...].astype(BF16), pick_cols[:, cols]).astype(BF16)
-        ts[:, :, cols] = dot(pick_rows[...], picked).astype(BF16).reshape(NR, 16, 256)
-    for step in range(NR):
-        peer = row_peer(step)
-        slot = tr.at[cp, lax.rem(rp, 2)]
-        here = jnp.logical_and(peer == rp, own_pair)
-
-        @pl.when(here)
-        def _():
-            pltpu.make_async_copy(ts.at[peer], slot, recv_sem.at[0]).start()
-
-        @pl.when(jnp.logical_not(here))
-        def _():
-            remote(ts.at[peer], slot, 0, {"rows": peer, "cols": half_row}).start()
+        ts[:, :, :, cols] = dot(pick_rows[...], picked).astype(BF16).reshape(NC, 2, 16, 256)
+    cols_exchange(ts, tr, 0)
 
     loads["base_cols"].wait()
     c, s = base_cols[0], base_cols[1]
@@ -299,7 +295,7 @@
     wc[512:1024, 512:1024] = c
     wc[0:512, 512:1024] = s
     wc[512:1024, 0:512] = -s
-    for name in ("wr", "turn_rows", "turn_source", "turn_lane"):
+    for name in ("wr", "turn_rows", "turn_cols"):
         loads[name].wait()
 
     lane128 = iota((1, 128), 1)
@@ -344,50 +340,53 @@
             got = dot(work_b[...].reshape(256, 512), wr[:, lanes])
             work_z[:, 16 * h:16 * h + 16, lanes] = got.astype(BF16).reshape(NR, 16, 256)
 
-    def mesh_send(src, dst, slot, at, r, g):
-        remote(src.at[r, g], dst.at[slot], at, {"rows": r, "cols": g}).start()
-
     def to_cols(send, recv, at):
-        def turn(step):
-            r = row_peer(step)
-            block = work_z[r]
-            block = jnp.concatenate([block[:, 128 * u:128 * u + 128] for u in range(4)], axis=0)
-            send[r] = block.T.reshape(NC, 16, 128)
-            return r
-
-        def others(step, _):
-            r = turn(step)
-            for away in range(NC):
-                g = col_peer(away)
-                remote(send.at[r, g], recv.at[cp, rp], at, {"rows": r, "cols": g}).start()
-            return 0
-
-        lax.fori_loop(1, NR, others, 0)
-        turn(0)
-        for away in range(1, NC):
-            g = col_peer(away)
-            remote(send.at[rp, g], recv.at[cp, rp], at, {"rows": rp, "cols": g}).start()
-        pltpu.make_async_copy(send.at[rp, cp], recv.at[cp, rp], recv_sem.at[at]).start()
+        for half in range(2):
+            def turn(step):
+                g = col_peer(step)
+                r = 2 * g + half
+                block = work_z[r]
+                block = jnp.concatenate([block[:, 128 * u:128 * u + 128] for u in range(4)], axis=0)
+                send[half, g] = block.T.reshape(NR, 8, 128)
+                return g
+
+            def others(step, _):
+                g = turn(step)
+                for away in range(NR):
+                    d = row_peer(away)
+                    remote(send.at[half, g, d], recv.at[half, cp, rp], at + half, {"rows": d, "cols": g}).start()
+                return 0
+
+            lax.fori_loop(1, NC, others, 0)
+            turn(0)
+            for away in range(1, NR):
+                d = row_peer(away)
+                remote(send.at[half, cp, d], recv.at[half, cp, rp], at + half, {"rows": d}).start()
+            tiles_kept(send.at[half, cp, rp], recv.at[half, cp, rp], send.at[half], at + half)
+
+    def tiles_kept(src, dst, send, at):
+        pltpu.make_async_copy(src, dst, recv_sem.at[at]).start()
+        first, second = send.shape[:2]
+        waits.append(lambda: sent(send.at[pl.ds(0, first - 1)], at))
+        waits.append(lambda: sent(send.at[0, pl.ds(0, second - 1)], at))
 
     def forward_cols(src):
         def first(at, _):
-            turned = []
-            for low in range(4):
-                t = at * 4 + low
-                values = []
-                for p in range(NC):
-                    tile = src[p, t].astype(F32)
-                    values.append((tile[:8], tile[8:]))
-                values = butterfly(values, 1)
+            parts = []
+            for p in range(NC):
+                parts.append(quad([src[p, at * 4 + low].astype(F32) for low in range(4)]))
+            halves = []
+            for u in range(2):
+                values = butterfly([(parts[p][2 * u], parts[p][2 * u + 1]) for p in range(NC)], 1)
                 for r in range(NC):
                     real, imag = values[r]
-                    cosine, sine = turn_source[0, r, t], turn_source[1, r, t]
+                    cosine, sine = turn_cols[0, r, at], turn_cols[1, r, at]
                     values[r] = (real * cosine - imag * sine, real * sine + imag * cosine)
-                turned.append(values)
+                halves.append(values)
             for r in range(NC):
                 for plane in range(2):
                     lanes = pl.ds(pl.multiple_of(at * 128 + 512 * plane, 128), 128)
-                    rows = quad([turned[low][r][plane] for low in range(4)])
+                    rows = [halves[u][r][plane] for u in range(2)]
                     work_d[r, :, lanes] = jnp.concatenate(rows, axis=0).astype(BF16)
             return 0
 
@@ -415,73 +414,76 @@
             first = tr[2 * e, :, :, src].reshape(32, 128).astype(F32)
             second = tr[2 * e + 1, :, :, src].reshape(32, 128).astype(F32)
             one, two = swap_halves(first, second)
-            tspace[2 * q, :, 128 * e:128 * e + 128] = one
-            tspace[2 * q + 1, :, 128 * e:128 * e + 128] = two
-
-    arrived(rd1, 3)
-    forward_cols(rd1)
-    for part in range(4):
-        lanes = slice(256 * part, 256 * part + 256)
-        kept = slice(256 * (part % 2), 256 * (part % 2) + 256)
-        space = dot(work_d[...].reshape(256, 1024), wc[:, lanes])
-        work_s[:, lanes] = (space * tspace[:, :, kept].reshape(256, 256)).astype(BF16)
-    for part in range(4):
-        lanes = slice(256 * part, 256 * part + 256)
-        work_f[:, :, lanes] = dot_nt(work_s[...], wc[lanes, :]).reshape(NC, 32, 256)
-
-    def last_cols(at, _):
-        re = pl.ds(pl.multiple_of(at * 128, 128), 128)
-        im = pl.ds(pl.multiple_of(at * 128 + 512, 128), 128)
-        parts = []
-        for u in range(4):
-            values = []
-            for r in range(NC):
-                real, imag = work_f[r, 8 * u:8 * u + 8, re], work_f[r, 8 * u:8 * u + 8, im]
-                cosine, sine = turn_lane[0, r, at], turn_lane[1, r, at]
-                values.append((real * cosine + imag * sine, imag * cosine - real * sine))
-            parts.append(butterfly(values, -1))
-        for q in range(NC):
-            reals = quad([parts[u][q][0] for u in range(4)])
-            imags = quad([parts[u][q][1] for u in range(4)])
-            for low in range(4):
-                sm2[at * 4 + low, q] = jnp.concatenate([reals[low], imags[low]], axis=0).astype(BF16)
-        return 0
-
-    lax.fori_loop(0, 4, last_cols, 0)
-
-    def send_back(step, _):
-        t = row_peer(step)
-        for away in range(NC):
+            tspace[:, 2 * q, :, 128 * e:128 * e + 128] = one.reshape(2, 16, 128)
+            tspace[:, 2 * q + 1, :, 128 * e:128 * e + 128] = two.reshape(2, 16, 128)
+
+    for half in range(2):
+        arrived(rd1.at[half], 3 + half)
+        forward_cols(rd1.at[half])
+        for part in range(4):
+            lanes = slice(256 * part, 256 * part + 256)
+            kept = slice(256 * (part % 2), 256 * (part % 2) + 256)
+            space = dot(work_d[...].reshape(128, 1024), wc[:, lanes])
+            work_s[:, lanes] = (space * tspace[half, :, :, kept].reshape(128, 256)).astype(BF16)
+        for part in range(4):
+            lanes = slice(256 * part, 256 * part + 256)
+            work_f[:, :, lanes] = dot_nt(work_s[...], wc[lanes, :]).reshape(NC, 16, 256)
+
+        def last_cols(at, _):
+            re = pl.ds(pl.multiple_of(at * 128, 128), 128)
+            im = pl.ds(pl.multiple_of(at * 128 + 512, 128), 128)
+            parts = []
+            for u in range(2):
+                values = []
+                for r in range(NC):
+                    real, imag = work_f[r, 8 * u:8 * u + 8, re], work_f[r, 8 * u:8 * u + 8, im]
+                    cosine, sine = turn_cols[0, r, at], turn_cols[1, r, at]
+                    values.append((real * cosine + imag * sine, imag * cosine - real * sine))
+                parts.append(butterfly(values, -1))
+            for q in range(NC):
+                tiles = quad([parts[0][q][0], parts[0][q][1], parts[1][q][0], parts[1][q][1]])
+                for low in range(4):
+                    sm2[half, at * 4 + low, q] = tiles[low].astype(BF16)
+            return 0
+
+        lax.fori_loop(0, 4, last_cols, 0)
+
+        def send_back(step, _):
+            t = row_peer(step)
+            for away in range(NC):
+                g = col_peer(away)
+                remote(sm2.at[half, t, g], rb2.at[half, cp, rp], 11 + half, {"rows": t, "cols": g}).start()
+            return 0
+
+        lax.fori_loop(1, NR, send_back, 0)
+        for away in range(1, NC):
             g = col_peer(away)
-            remote(sm2.at[t, g], rb2.at[rp, cp], 4, {"rows": t, "cols": g}).start()
-        return 0
-
-    lax.fori_loop(1, NR, send_back, 0)
-    for away in range(1, NC):
-        g = col_peer(away)
-        remote(sm2.at[rp, g], rb2.at[rp, cp], 4, {"rows": rp, "cols": g}).start()
-    pltpu.make_async_copy(sm2.at[rp, cp], rb2.at[rp, cp], recv_sem.at[4]).start()
-    arrived(rb2, 4)
-
-    def untile(s, _):
-        block = rb2[s].reshape(128, 128).T
-        for u in range(4):
-            work_z[s, :, 128 * u:128 * u + 128] = block[32 * u:32 * u + 32]
-        return 0
-
-    lax.fori_loop(0, NR, untile, 0)
-    for h in range(2):
+            remote(sm2.at[half, rp, g], rb2.at[half, cp, rp], 11 + half, {"cols": g}).start()
+        tiles_kept(sm2.at[half, rp, cp], rb2.at[half, cp, rp], sm2.at[half], 11 + half)
+
+    for half in range(2):
+        arrived(rb2.at[half], 11 + half)
+
+        def untile(g, _):
+            block = rb2[half, g].reshape(128, 128).T
+            for u in range(4):
+                work_y[g, :, 128 * u:128 * u + 128] = block[32 * u:32 * u + 32]
+            return 0
+
+        lax.fori_loop(0, NC, untile, 0)
         for part in range(2):
             lanes = slice(256 * part, 256 * part + 256)
-            rows = work_z[:, 16 * h:16 * h + 16, :].reshape(256, 512)
-            work_r[:, :, lanes] = dot_nt(rows, wr[lanes, :]).reshape(NR, 16, 256)
+            got = dot_nt(work_y[...].reshape(256, 512), wr[lanes, :])
+            work_r[half, :, :, lanes] = got.reshape(NC, 32, 256)
+    for h in range(2):
+        crow = slice(16 * h, 16 * h + 16)
 
         def sources(at, _):
             half = pl.multiple_of(at * 128, 128)
             re, im = pl.ds(half, 128), pl.ds(half + 256, 128)
             values = []
             for r in range(NR):
-                real, imag = work_r[r, :, re], work_r[r, :, im]
+                real, imag = work_r[r % 2, r // 2, crow, re], work_r[r % 2, r // 2, crow, im]
                 cosine, sine = turn_rows[0, r, :, re], turn_rows[1, r, :, re]
                 values.append((real * cosine + imag * sine, imag * cosine - real * sine))
             values = butterfly(values, -1)
@@ -512,61 +514,34 @@
         arrived(rb3.at[h], 7 + h)
         forward_rows(rb3.at[h], h)
     to_cols(sm3, rd3, 9)
-    arrived(rd3, 9)
-    forward_cols(rd3)
-    for part in range(4):
-        lanes = slice(256 * part, 256 * part + 256)
-        work_f[:, :, lanes] = dot(work_d[...].reshape(256, 1024), wc[:, lanes]).reshape(NC, 32, 256)
+    for half in range(2):
+        arrived(rd3.at[half], 9 + half)
+        forward_cols(rd3.at[half])
+        for part in range(4):
+            lanes = slice(256 * part, 256 * part + 256)
+            work_f[:, :, lanes] = dot(work_d[...].reshape(128, 1024), wc[:, lanes]).reshape(NC, 16, 256)
+        for plane in range(2):
+            for q in range(4):
+                for e in range(4):
+                    src = slice(512 * plane + 128 * e, 512 * plane + 128 * e + 128)
+                    lanes_to = slice(512 * plane + 128 * q, 512 * plane + 128 * q + 128)
+                    one, two = swap_halves(work_f[2 * q, :, src], work_f[2 * q + 1, :, src])
+                    fs[half, 2 * e, :, lanes_to] = one.astype(BF16)
+                    fs[half, 2 * e + 1, :, lanes_to] = two.astype(BF16)
+        cols_exchange(fs.at[half], rf.at[half], 13 + half)
+    for half in range(2):
+        arrived(rf.at[half], 13 + half)
+        for plane in range(2):
+            lanes = slice(512 * plane, 512 * plane + 512)
+            ordered = dot_nt(rf[half, :, :, lanes].reshape(128, 512), pick_cols[...])
+            work_o[plane, 128 * half:128 * half + 128, :] = ordered.astype(BF16)
     for plane in range(2):
-        for q in range(4):
-            for e in range(4):
-                src = slice(512 * plane + 128 * e, 512 * plane + 128 * e + 128)
-                lanes_to = slice(512 * plane + 128 * q, 512 * plane + 128 * q + 128)
-                one, two = swap_halves(work_f[2 * q, :, src], work_f[2 * q + 1, :, src])
-                fs[2 * e, :, lanes_to] = one.astype(BF16)
-                fs[2 * e + 1, :, lanes_to] = two.astype(BF16)
-    for h in range(2):
-        for step in range(NC):
-            peer = col_peer(step)
-            target = 2 * cp + h
-            here = jnp.logical_and(peer == cp, target == rp)
-            src = fs.at[peer, pl.ds(16 * h, 16)]
-
-            @pl.when(here)
-            def _():
-                pltpu.make_async_copy(src, rf.at[rp], recv_sem.at[10]).start()
-
-            @pl.when(jnp.logical_not(here))
-            def _():
-                remote(src, rf.at[rp], 10, {"rows": target, "cols": peer}).start()
-    arrived(rf, 10)
-    for plane in range(2):
-        ordered = dot_nt(rf[:, :, 512 * plane:512 * plane + 512].reshape(256, 512), pick_cols[...])
-        space = dot(back_rows[...], ordered.astype(BF16))
-        out[plane] = space * trans[...]
-        pltpu.make_async_copy(out.at[plane], out_h.at[plane], in_sem.at[9 + plane]).start()
-
-    for h in range(2):
-        halo_sent(spec_h.at[:, :, pl.ds(256 * h, 256)], h)
-        halo_sent(ra3.at[h], 2 + h)
-        for at, src in ((1, sa1), (5, sb2), (7, sa3)):
-            sent(src.at[h, pl.ds(0, NR - 1)], at + h)
-    for at, src in ((3, sm1), (4, sm2), (9, sm3)):
-        sent(src.at[pl.ds(0, NR - 1)], at)
-        sent(src.at[0, pl.ds(0, NC - 1)], at)
-
-    @pl.when(own_pair)
-    def _():
-        sent(ts.at[pl.ds(0, 15)], 0)
-        sent(rf.at[pl.ds(0, 15)], 10)
-
-    @pl.when(jnp.logical_not(own_pair))
-    def _():
-        sent(ts, 0)
-        sent(rf, 10)
-
-    for plane in range(2):
-        pltpu.make_async_copy(out.at[plane], out_h.at[plane], in_sem.at[9 + plane]).wait()
+        out[plane] = dot(back_rows[...], work_o[plane]) * trans[...]
+        result = pltpu.make_async_copy(out.at[plane], out_h.at[plane], in_sem.at[9 + plane])
+        result.start()
+        waits.append(result.wait)
+
+    finish()
 
 
 def on_device(spectrum, diffraction, order_mask, phases, transmission, shifts):
@@ -592,25 +567,27 @@
             vmem(F32, 2, 512, 256),
             vmem(BF16, 1024, 1024),
             vmem(BF16, 512, 512), vmem(BF16, 256, 256), vmem(BF16, 256, 256),
-            vmem(F32, NC, 32, 512),
+            vmem(F32, 2, NC, 16, 512),
             vmem(BF16, NR, 16, 512),
             vmem(BF16, NR, 32, 512),
-            vmem(F32, NR, 16, 512),
-            vmem(BF16, NC, 32, 1024),
-            vmem(BF16, 256, 1024),
-            vmem(F32, NC, 32, 1024),
+            vmem(BF16, NC, 32, 512),
+            vmem(F32, 2, NC, 32, 512),
+            vmem(BF16, NC, 16, 1024),
+            vmem(BF16, 128, 1024),
+            vmem(F32, NC, 16, 1024),
+            vmem(BF16, 2, 256, 512),
             vmem(BF16, *halves), vmem(BF16, *halves),
-            vmem(BF16, NR, NC, 16, 128), vmem(BF16, NC, NR, 16, 128),
-            vmem(BF16, NR, NC, 16, 128), vmem(BF16, NR, NC, 16, 128),
+            vmem(BF16, 2, NC, NR, 8, 128), vmem(BF16, 2, NC, NR, 8, 128),
+            vmem(BF16, 2, NR, NC, 8, 128), vmem(BF16, 2, NC, NR, 8, 128),
             vmem(BF16, *halves), vmem(BF16, *halves),
             vmem(BF16, *halves), vmem(BF16, *halves),
             vmem(BF16, *halves), vmem(BF16, *halves),
-            vmem(BF16, NR, NC, 16, 128), vmem(BF16, NC, NR, 16, 128),
-            vmem(BF16, NC, 32, 1024), vmem(BF16, NR, 16, 1024),
-            vmem(BF16, NR, 16, 512), vmem(BF16, NC, 2, 16, 512),
+            vmem(BF16, 2, NC, NR, 8, 128), vmem(BF16, 2, NC, NR, 8, 128),
+            vmem(BF16, 2, NC, 16, 1024), vmem(BF16, 2, NC, 16, 1024),
+            vmem(BF16, NC, 2, 16, 512), vmem(BF16, NC, 2, 16, 512),
             pltpu.SemaphoreType.DMA((11,)),
-            pltpu.SemaphoreType.DMA((11,)),
-            pltpu.SemaphoreType.DMA((11,)),
+            pltpu.SemaphoreType.DMA((15,)),
+            pltpu.SemaphoreType.DMA((15,)),
             pltpu.SemaphoreType.DMA((4, 4)),
             pltpu.SemaphoreType.REGULAR,
         ],

time: 115 us -> 93.1 us (0.81)
  the two profiles are of different devices: /device:TPU:49 before, /device:TPU:1 now
where the time goes in v3:
time: 93.1 us; the launch traced here: 93 us
  Pallas kernels  90.7 us (97%)
  local copies, waits for them, and re-layouts  2.26 us (2%)
    pallas_call x1, Pallas kernels, on_device(): pl.pallas_call(kernel, out_shape=jax.ShapeDtypeStruct((2, 256, 512), F32)...  90.7 us
    unnamed x1, local copies, waits for them, and re-layouts  2.26 us

profile of v3, /device:TPU:1, one launch (start us, length us, event | category | flops | bytes accessed | tf_op | source)
XLA Modules:
  0.0 93.0 jit_solution(1087051137319500995)
XLA Ops:
  0.0 90.7 %shard_map.100 = f32[2,256,512]{2,1,0:T(8,128)} custom-call(s32[2]{0:T(128)} %shifts.1, s32[2,3]{1,0:T(2,128)} %mask.1, bf16[2,256,512]{2,1,0:T(8,128)(2,1)} %spec_h.1, bf16[2,2,3,128,128]{4,3,2,1,0:T(8,128)(2,1)} %diff_h.1, f32[2,256,512]{2,1,0:T(8,128)} %phases_h.1, f32[256,512]{1,0:T(8,128)} %trans_h.1, bf16[512,512]{1,0:T(8,128)(2,1)} %constant.8.clone.base_rows_h, ...), custom_call_target="tpu_custom_call" | custom-call | tf_op jit(solution)/shard_map/pallas_call | solution.py:557
  90.7 2.3 %copy.12 = f32[2,256,512]{2,1,0:T(8,128)} copy(f32[2,256,512]{2,1,0:T(8,128)} %shard_map.100) | data formatting | bytes 2097152

commit v4 on v3

--- a/solution.py
+++ b/solution.py
@@ -13,6 +13,27 @@
 NR = 16
 NC = 8
 FULL = 4096
+
+
+def ring(step):
+    return min(step, 4 - step)
+
+
+def depth(high, low):
+    return (0, 1, 2, 1)[2 * high + low]
+
+
+ROW_STEPS = sorted(
+    ((z, x, c) for z in range(2) for x in range(4) for c in range(2)),
+    key=lambda o: -(8 * (o[0] + ring(o[1])) + o[2]),
+)
+COL_STEPS = sorted(
+    ((z, y) for z in range(2) for y in range(4)), key=lambda o: -(2 * o[0] + ring(o[1]))
+)
+PAIR_STEPS = sorted(
+    ((r, c) for r in ROW_STEPS for c in COL_STEPS),
+    key=lambda p: -(8 * (depth(p[1][0], p[0][0]) + ring(p[0][1]) + ring(p[1][1])) + p[0][2]),
+)
 
 
 def tables():
@@ -109,11 +130,19 @@
     rp = lax.axis_index("rows")
     cp = lax.axis_index("cols")
 
-    def row_peer(step):
+    z_lo, x, core = lax.div(rp, 8), lax.rem(lax.div(rp, 2), 4), lax.rem(rp, 2)
+    z_hi, y = lax.div(cp, 4), lax.rem(cp, 4)
+
+    def row_at(step):
         return lax.rem(rp + step, NR)
 
-    def col_peer(step):
+    def col_at(step):
         return lax.rem(cp + step, NC)
+
+    row_peer = {
+        o: lax.rem(z_lo + o[0], 2) * 8 + lax.rem(x + o[1], 4) * 2 + lax.rem(core + o[2], 2) for o in ROW_STEPS
+    }
+    col_peer = {o: lax.rem(z_hi + o[0], 2) * 4 + lax.rem(y + o[1], 4) for o in COL_STEPS}
 
     waits = []
 
@@ -122,10 +151,22 @@
             wait()
 
     barrier = pltpu.get_barrier_semaphore()
-    for step in range(1, NR):
-        pl.semaphore_signal(barrier, inc=1, device_id={"rows": row_peer(step)})
-    for step in range(1, NC):
-        pl.semaphore_signal(barrier, inc=1, device_id={"cols": col_peer(step)})
+    for step in (1, NR - 1):
+        pl.semaphore_signal(barrier, inc=1, device_id={"rows": row_at(step)})
+    for step in (1, NC - 1):
+        pl.semaphore_signal(barrier, inc=1, device_id={"cols": col_at(step)})
+
+    rounds = (("rows", 1), ("rows", 2), ("rows", 4), ("cols", 1), ("cols", 2), ("cols", 4))
+
+    def tell(which):
+        axis, reach = rounds[which]
+        count, at = (NR, row_at) if axis == "rows" else (NC, col_at)
+        for step in sorted({reach, count - reach}):
+            pl.semaphore_signal(ready_sem.at[which], inc=1, device_id={axis: at(step)})
+
+    def told(which):
+        axis, reach = rounds[which]
+        pl.semaphore_wait(ready_sem.at[which], 1 if 2 * reach == NC and axis == "cols" else 2)
 
     loads = {}
     for at, (name, src, dst) in enumerate((
@@ -142,18 +183,26 @@
         )
 
     def rows_exchange(src, dst, at):
-        for step in range(1, NR):
-            peer = row_peer(step)
+        for step in ROW_STEPS[:-1]:
+            peer = row_peer[step]
             remote(src.at[peer], dst.at[rp], at, {"rows": peer}).start()
         pltpu.make_async_copy(src.at[rp], dst.at[rp], recv_sem.at[at]).start()
         waits.append(lambda: sent(src.at[pl.ds(0, NR - 1)], at))
 
     def cols_exchange(src, dst, at):
-        for step in range(1, NC):
-            peer = col_peer(step)
+        for step in COL_STEPS[:-1]:
+            peer = col_peer[step]
             remote(src.at[peer], dst.at[cp], at, {"cols": peer}).start()
         pltpu.make_async_copy(src.at[cp], dst.at[cp], recv_sem.at[at]).start()
         waits.append(lambda: sent(src.at[pl.ds(0, NC - 1)], at))
+
+    def tiles_exchange(src, dst, at):
+        for row_step, col_step in PAIR_STEPS[:-1]:
+            d, g = row_peer[row_step], col_peer[col_step]
+            remote(src.at[g, d], dst.at[cp, rp], at, {"rows": d, "cols": g}).start()
+        pltpu.make_async_copy(src.at[cp, rp], dst.at[cp, rp], recv_sem.at[at]).start()
+        waits.append(lambda: sent(src.at[pl.ds(0, NC - 1)], at))
+        waits.append(lambda: sent(src.at[0, pl.ds(0, NR - 1)], at))
 
     def arrived(dst, at):
         pltpu.make_async_copy(dst, dst, recv_sem.at[at]).wait()
@@ -240,12 +289,10 @@
         high0[...] = jnp.zeros_like(high0)
         high1[...] = jnp.zeros_like(high1)
 
-    pl.semaphore_wait(barrier, NR - 1 + NC - 1)
+    pl.semaphore_wait(barrier, 4)
     for h in range(2):
         halo_start(spec_h.at[:, :, pl.ds(256 * h, 256)], low0.at[h], high0.at[h], h)
-    for step in range(1, NC):
-        pl.semaphore_signal(ready_sem, inc=1, device_id={"cols": col_peer(step)})
-
+    tell(0)
     loads["phases"].wait()
 
     def phase0(at, _):
@@ -255,7 +302,13 @@
         trig0[1, rows, :] = sine
         return 0
 
-    lax.fori_loop(0, 8, phase0, 0)
+    lax.fori_loop(0, 3, phase0, 0)
+    told(0)
+    tell(1)
+    lax.fori_loop(3, 6, phase0, 0)
+    told(1)
+    tell(2)
+    lax.fori_loop(6, 8, phase0, 0)
     loads["spec"].wait()
 
     for h in range(2):
@@ -272,9 +325,13 @@
             wave_im = (real * sine + imag * cosine).astype(BF16)
             sa1[h, 8 * part:8 * part + 8, :, 0:256] = wave_re.T.reshape(8, 16, 256)
             sa1[h, 8 * part:8 * part + 8, :, 256:512] = wave_im.T.reshape(8, 16, 256)
+        if h == 0:
+            told(2)
+            tell(3)
         rows_exchange(sa1.at[h], rb1.at[h], 1 + h)
 
-    pl.semaphore_wait(ready_sem, NC - 1)
+    told(3)
+    tell(4)
 
     lane = iota((512, 512), 1)
     pick_cols[...] = one_hot(iota((512, 512), 0) == (lane & 63) * 8 + (lane >> 6))
@@ -282,11 +339,14 @@
     pick_rows[...] = one_hot(b == (a & 15) * 16 + (a >> 4))
     back_rows[...] = one_hot(b == (a & 1) * 128 + ((a & 15) >> 1) * 16 + (a >> 4))
 
+    told(4)
+    tell(5)
     loads["trans"].wait()
     for half in range(2):
         cols = pl.ds(half * 256, 256)
         picked = dot(trans[...].astype(BF16), pick_cols[:, cols]).astype(BF16)
         ts[:, :, :, cols] = dot(pick_rows[...], picked).astype(BF16).reshape(NC, 2, 16, 256)
+    told(5)
     cols_exchange(ts, tr, 0)
 
     loads["base_cols"].wait()
@@ -342,33 +402,14 @@
 
     def to_cols(send, recv, at):
         for half in range(2):
-            def turn(step):
-                g = col_peer(step)
-                r = 2 * g + half
-                block = work_z[r]
+            def turn(g, _):
+                block = work_z[2 * g + half]
                 block = jnp.concatenate([block[:, 128 * u:128 * u + 128] for u in range(4)], axis=0)
                 send[half, g] = block.T.reshape(NR, 8, 128)
-                return g
-
-            def others(step, _):
-                g = turn(step)
-                for away in range(NR):
-                    d = row_peer(away)
-                    remote(send.at[half, g, d], recv.at[half, cp, rp], at + half, {"rows": d, "cols": g}).start()
                 return 0
 
-            lax.fori_loop(1, NC, others, 0)
-            turn(0)
-            for away in range(1, NR):
-                d = row_peer(away)
-                remote(send.at[half, cp, d], recv.at[half, cp, rp], at + half, {"rows": d}).start()
-            tiles_kept(send.at[half, cp, rp], recv.at[half, cp, rp], send.at[half], at + half)
-
-    def tiles_kept(src, dst, send, at):
-        pltpu.make_async_copy(src, dst, recv_sem.at[at]).start()
-        first, second = send.shape[:2]
-        waits.append(lambda: sent(send.at[pl.ds(0, first - 1)], at))
-        waits.append(lambda: sent(send.at[0, pl.ds(0, second - 1)], at))
+            lax.fori_loop(0, NC, turn, 0)
+            tiles_exchange(send.at[half], recv.at[half], at + half)
 
     def forward_cols(src):
         def first(at, _):
@@ -443,23 +484,12 @@
             for q in range(NC):
                 tiles = quad([parts[0][q][0], parts[0][q][1], parts[1][q][0], parts[1][q][1]])
                 for low in range(4):
-                    sm2[half, at * 4 + low, q] = tiles[low].astype(BF16)
+                    sm2[half, q, at * 4 + low] = tiles[low].astype(BF16)
             return 0
 
         lax.fori_loop(0, 4, last_cols, 0)
 
-        def send_back(step, _):
-            t = row_peer(step)
-            for away in range(NC):
-                g = col_peer(away)
-                remote(sm2.at[half, t, g], rb2.at[half, cp, rp], 11 + half, {"rows": t, "cols": g}).start()
-            return 0
-
-        lax.fori_loop(1, NR, send_back, 0)
-        for away in range(1, NC):
-            g = col_peer(away)
-            remote(sm2.at[half, rp, g], rb2.at[half, cp, rp], 11 + half, {"cols": g}).start()
-        tiles_kept(sm2.at[half, rp, cp], rb2.at[half, cp, rp], sm2.at[half], 11 + half)
+        tiles_exchange(sm2.at[half], rb2.at[half], 11 + half)
 
     for half in range(2):
         arrived(rb2.at[half], 11 + half)
@@ -536,7 +566,7 @@
             ordered = dot_nt(rf[half, :, :, lanes].reshape(128, 512), pick_cols[...])
             work_o[plane, 128 * half:128 * half + 128, :] = ordered.astype(BF16)
     for plane in range(2):
-        out[plane] = dot(back_rows[...], work_o[plane]) * trans[...]
+        out[plane] = dot(back_rows[...], work_o[plane]).astype(BF16)
         result = pltpu.make_async_copy(out.at[plane], out_h.at[plane], in_sem.at[9 + plane])
         result.start()
         waits.append(result.wait)
@@ -554,13 +584,13 @@
         return pltpu.VMEM(shape, kind)
 
     halves = (2, NR, 16, 512)
-    return pl.pallas_call(
+    space = pl.pallas_call(
         kernel,
-        out_shape=jax.ShapeDtypeStruct((2, 256, 512), F32),
+        out_shape=jax.ShapeDtypeStruct((2, 256, 512), BF16),
         in_specs=[smem, smem] + [anywhere] * len(operands),
         out_specs=anywhere,
         scratch_shapes=[pltpu.VMEM(x.shape, x.dtype) for x in operands] + [
-            vmem(F32, 2, 256, 512),
+            vmem(BF16, 2, 256, 512),
             vmem(BF16, 2, 2, 256, 256), vmem(BF16, 2, 2, 256, 256),
             vmem(BF16, 2, 3, 512, 512),
             vmem(F32, 2, 256, 512),
@@ -578,7 +608,7 @@
             vmem(BF16, 2, 256, 512),
             vmem(BF16, *halves), vmem(BF16, *halves),
             vmem(BF16, 2, NC, NR, 8, 128), vmem(BF16, 2, NC, NR, 8, 128),
-            vmem(BF16, 2, NR, NC, 8, 128), vmem(BF16, 2, NC, NR, 8, 128),
+            vmem(BF16, 2, NC, NR, 8, 128), vmem(BF16, 2, NC, NR, 8, 128),
             vmem(BF16, *halves), vmem(BF16, *halves),
             vmem(BF16, *halves), vmem(BF16, *halves),
             vmem(BF16, *halves), vmem(BF16, *halves),
@@ -589,12 +619,13 @@
             pltpu.SemaphoreType.DMA((15,)),
             pltpu.SemaphoreType.DMA((15,)),
             pltpu.SemaphoreType.DMA((4, 4)),
-            pltpu.SemaphoreType.REGULAR,
+            pltpu.SemaphoreType.REGULAR((6,)),
         ],
         compiler_params=pltpu.CompilerParams(
             collective_id=0, has_side_effects=True, vmem_limit_bytes=60 * 1024 * 1024
         ),
     )(shifts, order_mask, *operands)
+    return space.astype(F32) * transmission[None]
 
 
 def solution(mesh):

time: 93.1 us -> 91.7 us (0.985)
  local copies, waits for them, and re-layouts: 2.26 us -> 0.01 us
  other arithmetic: 0 us -> 2.17 us
  Pallas kernels: 90.7 us -> 89.3 us
    unnamed x1 -> x2, local copies, waits for them, and re-layouts: 2.26 us -> 0.01 us
    mul x0 -> x1, other arithmetic: none -> 2.17 us  [on_device(): return space.astype(F32) * transmission[None]]
    pallas_call x1, Pallas kernels: 90.7 us -> 89.3 us  [on_device(): pl.pallas_call(kernel, out_shape=jax.ShapeDtypeStruct((2, 256, 512), BF16...]
where the time goes in v4:
time: 91.7 us; the launch traced here: 91.5 us
  Pallas kernels  89.3 us (97%)
  other arithmetic  2.17 us (2%)
    pallas_call x1, Pallas kernels, on_device(): pl.pallas_call(kernel, out_shape=jax.ShapeDtypeStruct((2, 256, 512), BF16...  89.3 us
    mul x1, other arithmetic, on_device(): return space.astype(F32) * transmission[None]  2.17 us

profile of v4, /device:TPU:1, one launch (start us, length us, event | category | flops | bytes accessed | tf_op | source)
XLA Modules:
  0.0 91.5 jit_solution(18429004015578660790)
XLA Ops:
  0.0 0.0 copy-start
  0.0 89.3 %shard_map.100 = bf16[2,256,512]{2,1,0:T(8,128)(2,1)} custom-call(s32[2]{0:T(128)} %shifts.1, s32[2,3]{1,0:T(2,128)} %mask.1, bf16[2,256,512]{2,1,0:T(8,128)(2,1)} %spec_h.1, bf16[2,2,3,128,128]{4,3,2,1,0:T(8,128)(2,1)} %diff_h.1, f32[2,256,512]{2,1,0:T(8,128)} %phases_h.1, f32[256,512]{1,0:T(8,128)} %trans_h.1, bf16[512,512]{1,0:T(8,128)(2,1)} %constant.8.clone.base_rows_h, ...), custom_call_target="tpu_custom_call" | custom-call | tf_op jit(solution)/shard_map/pallas_call | solution.py:587
  89.4 0.0 copy-done
  89.4 2.2 %convert_multiply_fusion = f32[2,256,512]{2,1,0:T(8,128)} fusion(bf16[2,256,512]{2,1,0:T(8,128)(2,1)} %shard_map.100, f32[256,512]{1,0:T(8,128)S(1)} %copy-done), kind=kLoop, calls=%fused_computation | loop fusion | flops 524288 | bytes 2097152 | tf_op jit(solution)/shard_map/mul | solution.py:628
Async XLA Ops:
  0.0 89.4 %copy-start = (f32[256,512]{1,0:T(8,128)S(1)}, f32[256,512]{1,0:T(8,128)}, u32[]{:S(2)}) copy-start(f32[256,512]{1,0:T(8,128)} %trans_h.1) | copy-start | bytes 1572868

commit v5 on v4

--- a/solution.py
+++ b/solution.py
@@ -46,15 +46,13 @@
     imaginary = at // 128 % 2 == 1
     c, s = circle(256, np.arange(256), row)
     base_rows = np.concatenate([np.where(imaginary, s, c), np.where(imaginary, c, -s)]) / 64.0
-    col = 256 * (at // 16 % 2) + 16 * (at // 32) + at % 16
-    base_cols = np.stack(circle(512, col, np.arange(512))) / 64.0
+    c, s = circle(256, np.arange(256), np.arange(256))
+    base_cols = np.block([[c, s], [-s, c]]) / 64.0
     turn_rows = np.stack(circle(FULL, np.arange(NR), np.arange(256)))[:, :, None, :]
-    turn_cols = np.stack(circle(FULL, np.arange(NC), col)).reshape(2, NC, 4, 1, 128)
     return (
         jnp.asarray(base_rows, BF16),
         jnp.asarray(base_cols, BF16),
         jnp.asarray(turn_rows, F32),
-        jnp.asarray(turn_cols, F32),
     )
 
 
@@ -120,10 +118,10 @@
 
 
 def kernel(
-    shifts, mask, spec_h, diff_h, phases_h, trans_h, base_rows_h, base_cols_h, turn_rows_h, turn_cols_h, out_h,
-    spec, diff, phases, trans, wr, base_cols, turn_rows, turn_cols, out,
-    low0, high0, dw, trig0, trig1, wc, pick_cols, pick_rows, back_rows, tspace,
-    work_b, work_z, work_y, work_r, work_d, work_s, work_f, work_o,
+    shifts, mask, spec_h, diff_h, phases_h, trans_h, base_rows_h, base_cols_h, turn_rows_h, out_h,
+    spec, diff, phases, trans, wr, wc, turn_rows, out,
+    low0, high0, dw, trig0, trig1, pick_cols, pick_rows, back_rows, tspace,
+    work_b, work_z, work_y, work_r, work_d, work_s, work_x, work_o,
     sa1, rb1, sm1, rd1, sm2, rb2, sb2, ra3, low1, high1, sa3, rb3, sm3, rd3, fs, rf, ts, tr,
     in_sem, send_sem, recv_sem, halo_sem, ready_sem,
 ):
@@ -172,7 +170,7 @@
     for at, (name, src, dst) in enumerate((
         ("diff", diff_h, diff), ("phases", phases_h, phases), ("spec", spec_h, spec),
         ("wr", base_rows_h, wr), ("turn_rows", turn_rows_h, turn_rows), ("trans", trans_h, trans),
-        ("base_cols", base_cols_h, base_cols), ("turn_cols", turn_cols_h, turn_cols),
+        ("wc", base_cols_h, wc),
     )):
         loads[name] = pltpu.make_async_copy(src, dst, in_sem.at[at])
         loads[name].start()
@@ -334,7 +332,7 @@
     tell(4)
 
     lane = iota((512, 512), 1)
-    pick_cols[...] = one_hot(iota((512, 512), 0) == (lane & 63) * 8 + (lane >> 6))
+    pick_cols[...] = one_hot(iota((512, 512), 0) == (lane & 31) * 16 + (lane >> 5))
     a, b = iota((256, 256), 0), iota((256, 256), 1)
     pick_rows[...] = one_hot(b == (a & 15) * 16 + (a >> 4))
     back_rows[...] = one_hot(b == (a & 1) * 128 + ((a & 15) >> 1) * 16 + (a >> 4))
@@ -349,37 +347,29 @@
     told(5)
     cols_exchange(ts, tr, 0)
 
-    loads["base_cols"].wait()
-    c, s = base_cols[0], base_cols[1]
-    wc[0:512, 0:512] = c
-    wc[512:1024, 512:1024] = c
-    wc[0:512, 512:1024] = s
-    wc[512:1024, 0:512] = -s
-    for name in ("wr", "turn_rows", "turn_cols"):
+    for name in ("wr", "wc", "turn_rows"):
         loads[name].wait()
 
     lane128 = iota((1, 128), 1)
-    low_half = lane128 < 64
-    even_group = (lane128 & 32) == 0
-
-    def swap_halves(first, second):
+
+    def swap(first, second, size):
+        even = (lane128 & size) == 0
         return (
-            jnp.where(low_half, first, pltpu.roll(second, 64, 1)),
-            jnp.where(low_half, pltpu.roll(first, 64, 1), second),
+            jnp.where(even, first, pltpu.roll(second, size, 1)),
+            jnp.where(even, pltpu.roll(first, 128 - size, 1), second),
         )
 
-    def swap_groups(first, second):
-        return (
-            jnp.where(even_group, first, pltpu.roll(second, 32, 1)),
-            jnp.where(even_group, pltpu.roll(first, 96, 1), second),
-        )
-
-    def quad(values):
-        p0, p2 = swap_halves(values[0], values[2])
-        p1, p3 = swap_halves(values[1], values[3])
-        b0, b1 = swap_groups(p0, p1)
-        b2, b3 = swap_groups(p2, p3)
-        return [b0, b1, b2, b3]
+    def crossed(values):
+        reach = len(values) // 2
+        while reach:
+            size = reach * (128 // len(values))
+            result = list(values)
+            for at in range(len(values)):
+                if at & reach == 0:
+                    result[at], result[at + reach] = swap(values[at], values[at + reach], size)
+            values = result
+            reach //= 2
+        return values
 
     def forward_rows(src, h):
         def first(at, _):
@@ -413,25 +403,23 @@
 
     def forward_cols(src):
         def first(at, _):
-            parts = []
+            lanes = pl.ds(pl.multiple_of(at * 128, 128), 128)
+            lanes2 = pl.ds(pl.multiple_of(at * 128 + 256, 128), 128)
             for p in range(NC):
-                parts.append(quad([src[p, at * 4 + low].astype(F32) for low in range(4)]))
-            halves = []
+                parts = crossed([src[p, at * 8 + low].astype(F32) for low in range(8)])
+                for k in range(8):
+                    work_x[k // 4, k // 2 % 2, 2 * p + k % 2] = parts[k]
             for u in range(2):
-                values = butterfly([(parts[p][2 * u], parts[p][2 * u + 1]) for p in range(NC)], 1)
-                for r in range(NC):
+                values = butterfly([(work_x[u, 0, p], work_x[u, 1, p]) for p in range(NR)], 1)
+                for r in range(NR):
                     real, imag = values[r]
-                    cosine, sine = turn_cols[0, r, at], turn_cols[1, r, at]
-                    values[r] = (real * cosine - imag * sine, real * sine + imag * cosine)
-                halves.append(values)
-            for r in range(NC):
-                for plane in range(2):
-                    lanes = pl.ds(pl.multiple_of(at * 128 + 512 * plane, 128), 128)
-                    rows = [halves[u][r][plane] for u in range(2)]
-                    work_d[r, :, lanes] = jnp.concatenate(rows, axis=0).astype(BF16)
+                    cosine, sine = turn_rows[0, r, :, lanes], turn_rows[1, r, :, lanes]
+                    rows = slice(8 * u, 8 * u + 8)
+                    work_d[r, rows, lanes] = real * cosine - imag * sine
+                    work_d[r, rows, lanes2] = real * sine + imag * cosine
             return 0
 
-        lax.fori_loop(0, 4, first, 0)
+        lax.fori_loop(0, 2, first, 0)
 
     def phase1(at, _):
         cols = pl.ds(pl.multiple_of(at * 128, 128), 128)
@@ -449,46 +437,44 @@
     banded(1)
 
     arrived(tr, 0)
-    for e in range(4):
+    for e in range(2):
         for q in range(4):
             src = slice(128 * q, 128 * q + 128)
-            first = tr[2 * e, :, :, src].reshape(32, 128).astype(F32)
-            second = tr[2 * e + 1, :, :, src].reshape(32, 128).astype(F32)
-            one, two = swap_halves(first, second)
-            tspace[:, 2 * q, :, 128 * e:128 * e + 128] = one.reshape(2, 16, 128)
-            tspace[:, 2 * q + 1, :, 128 * e:128 * e + 128] = two.reshape(2, 16, 128)
+            got = crossed([tr[4 * e + k, :, :, src].reshape(32, 128).astype(F32) for k in range(4)])
+            for k in range(4):
+                tspace[:, 4 * q + k, :, 128 * e:128 * e + 128] = got[k].reshape(2, 16, 128)
 
     for half in range(2):
         arrived(rd1.at[half], 3 + half)
         forward_cols(rd1.at[half])
-        for part in range(4):
+        rows = work_d[...].astype(BF16).reshape(256, 512)
+        for part in range(2):
             lanes = slice(256 * part, 256 * part + 256)
-            kept = slice(256 * (part % 2), 256 * (part % 2) + 256)
-            space = dot(work_d[...].reshape(128, 1024), wc[:, lanes])
-            work_s[:, lanes] = (space * tspace[half, :, :, kept].reshape(128, 256)).astype(BF16)
-        for part in range(4):
+            space = dot(rows, wc[:, lanes])
+            work_s[:, lanes] = (space * tspace[half].reshape(256, 256)).astype(BF16)
+        for part in range(2):
             lanes = slice(256 * part, 256 * part + 256)
-            work_f[:, :, lanes] = dot_nt(work_s[...], wc[lanes, :]).reshape(NC, 16, 256)
+            work_d[:, :, lanes] = dot_nt(work_s[...], wc[lanes, :]).reshape(NR, 16, 256)
 
         def last_cols(at, _):
             re = pl.ds(pl.multiple_of(at * 128, 128), 128)
-            im = pl.ds(pl.multiple_of(at * 128 + 512, 128), 128)
-            parts = []
+            im = pl.ds(pl.multiple_of(at * 128 + 256, 128), 128)
             for u in range(2):
                 values = []
-                for r in range(NC):
-                    real, imag = work_f[r, 8 * u:8 * u + 8, re], work_f[r, 8 * u:8 * u + 8, im]
-                    cosine, sine = turn_cols[0, r, at], turn_cols[1, r, at]
+                for r in range(NR):
+                    real, imag = work_d[r, 8 * u:8 * u + 8, re], work_d[r, 8 * u:8 * u + 8, im]
+                    cosine, sine = turn_rows[0, r, :, re], turn_rows[1, r, :, re]
                     values.append((real * cosine + imag * sine, imag * cosine - real * sine))
-                parts.append(butterfly(values, -1))
+                values = butterfly(values, -1)
+                for r in range(NR):
+                    work_x[u, 0, r], work_x[u, 1, r] = values[r]
             for q in range(NC):
-                tiles = quad([parts[0][q][0], parts[0][q][1], parts[1][q][0], parts[1][q][1]])
-                for low in range(4):
-                    sm2[half, q, at * 4 + low] = tiles[low].astype(BF16)
+                tiles = crossed([work_x[k // 4, k // 2 % 2, 2 * q + k % 2] for k in range(8)])
+                for low in range(8):
+                    sm2[half, q, at * 8 + low] = tiles[low].astype(BF16)
             return 0
 
-        lax.fori_loop(0, 4, last_cols, 0)
-
+        lax.fori_loop(0, 2, last_cols, 0)
         tiles_exchange(sm2.at[half], rb2.at[half], 11 + half)
 
     for half in range(2):
@@ -547,17 +533,17 @@
     for half in range(2):
         arrived(rd3.at[half], 9 + half)
         forward_cols(rd3.at[half])
-        for part in range(4):
-            lanes = slice(256 * part, 256 * part + 256)
-            work_f[:, :, lanes] = dot(work_d[...].reshape(128, 1024), wc[:, lanes]).reshape(NC, 16, 256)
+        rows = work_d[...].astype(BF16).reshape(256, 512)
         for plane in range(2):
+            lanes = slice(256 * plane, 256 * plane + 256)
+            work_d[:, :, lanes] = dot(rows, wc[:, lanes]).reshape(NR, 16, 256)
             for q in range(4):
-                for e in range(4):
-                    src = slice(512 * plane + 128 * e, 512 * plane + 128 * e + 128)
+                for e in range(2):
+                    src = slice(256 * plane + 128 * e, 256 * plane + 128 * e + 128)
                     lanes_to = slice(512 * plane + 128 * q, 512 * plane + 128 * q + 128)
-                    one, two = swap_halves(work_f[2 * q, :, src], work_f[2 * q + 1, :, src])
-                    fs[half, 2 * e, :, lanes_to] = one.astype(BF16)
-                    fs[half, 2 * e + 1, :, lanes_to] = two.astype(BF16)
+                    got = crossed([work_d[4 * q + k, :, src] for k in range(4)])
+                    for k in range(4):
+                        fs[half, 4 * e + k, :, lanes_to] = got[k].astype(BF16)
         cols_exchange(fs.at[half], rf.at[half], 13 + half)
     for half in range(2):
         arrived(rf.at[half], 13 + half)
@@ -595,16 +581,15 @@
             vmem(BF16, 2, 3, 512, 512),
             vmem(F32, 2, 256, 512),
             vmem(F32, 2, 512, 256),
-            vmem(BF16, 1024, 1024),
             vmem(BF16, 512, 512), vmem(BF16, 256, 256), vmem(BF16, 256, 256),
-            vmem(F32, 2, NC, 16, 512),
+            vmem(F32, 2, NR, 16, 256),
             vmem(BF16, NR, 16, 512),
             vmem(BF16, NR, 32, 512),
             vmem(BF16, NC, 32, 512),
             vmem(F32, 2, NC, 32, 512),
-            vmem(BF16, NC, 16, 1024),
-            vmem(BF16, 128, 1024),
-            vmem(F32, NC, 16, 1024),
+            vmem(F32, NR, 16, 512),
+            vmem(BF16, 256, 512),
+            vmem(F32, 2, 2, NR, 8, 128),
             vmem(BF16, 2, 256, 512),
             vmem(BF16, *halves), vmem(BF16, *halves),
             vmem(BF16, 2, NC, NR, 8, 128), vmem(BF16, 2, NC, NR, 8, 128),

time: 91.7 us -> 90.1 us (0.983)
  Pallas kernels: 89.3 us -> 87.7 us
    pallas_call x1, Pallas kernels: 89.3 us -> 87.7 us  [on_device(): pl.pallas_call(kernel, out_shape=jax.ShapeDtypeStruct((2, 256, 512), BF16...]
where the time goes in v5:
time: 90.1 us; the launch traced here: 89.9 us
  Pallas kernels  87.7 us (97%)
  other arithmetic  2.17 us (2%)
    pallas_call x1, Pallas kernels, on_device(): pl.pallas_call(kernel, out_shape=jax.ShapeDtypeStruct((2, 256, 512), BF16...  87.7 us
    mul x1, other arithmetic, on_device(): return space.astype(F32) * transmission[None]  2.17 us

profile of v5, /device:TPU:1, one launch (start us, length us, event | category | flops | bytes accessed | tf_op | source)
XLA Modules:
  0.0 89.9 jit_solution(11131056905447119264)
XLA Ops:
  0.0 0.0 copy-start
  0.0 87.7 %shard_map.91 = bf16[2,256,512]{2,1,0:T(8,128)(2,1)} custom-call(s32[2]{0:T(128)} %shifts.1, s32[2,3]{1,0:T(2,128)} %mask.1, bf16[2,256,512]{2,1,0:T(8,128)(2,1)} %spec_h.1, bf16[2,2,3,128,128]{4,3,2,1,0:T(8,128)(2,1)} %diff_h.1, f32[2,256,512]{2,1,0:T(8,128)} %phases_h.1, f32[256,512]{1,0:T(8,128)} %trans_h.1, bf16[512,512]{1,0:T(8,128)(2,1)} %constant.6.clone.base_rows_h, ...), custom_call_target="tpu_custom_call" | custom-call | tf_op jit(solution)/shard_map/pallas_call | solution.py:573
  87.7 0.0 copy-done
  87.7 2.2 %convert_multiply_fusion = f32[2,256,512]{2,1,0:T(8,128)} fusion(bf16[2,256,512]{2,1,0:T(8,128)(2,1)} %shard_map.91, f32[256,512]{1,0:T(8,128)S(1)} %copy-done), kind=kLoop, calls=%fused_computation | loop fusion | flops 524288 | bytes 2097152 | tf_op jit(solution)/shard_map/mul | solution.py:613
Async XLA Ops:
  0.0 87.7 %copy-start = (f32[256,512]{1,0:T(8,128)S(1)}, f32[256,512]{1,0:T(8,128)}, u32[]{:S(2)}) copy-start(f32[256,512]{1,0:T(8,128)} %trans_h.1) | copy-start | bytes 1572868

commit v6 on v5

--- a/solution.py
+++ b/solution.py
@@ -13,6 +13,7 @@
 NR = 16
 NC = 8
 FULL = 4096
+CHUNKS = 4
 
 
 def ring(step):
@@ -46,13 +47,17 @@
     imaginary = at // 128 % 2 == 1
     c, s = circle(256, np.arange(256), row)
     base_rows = np.concatenate([np.where(imaginary, s, c), np.where(imaginary, c, -s)]) / 64.0
-    c, s = circle(256, np.arange(256), np.arange(256))
+    at = np.arange(256)
+    col = 128 * (at // 8 % 2) + 64 * (at // 128) + 8 * (at // 16 % 8) + at % 8
+    c, s = circle(256, col, np.arange(256))
     base_cols = np.block([[c, s], [-s, c]]) / 64.0
     turn_rows = np.stack(circle(FULL, np.arange(NR), np.arange(256)))[:, :, None, :]
+    turn_cols = np.stack(circle(FULL, np.arange(NR), col))[:, :, None, :]
     return (
         jnp.asarray(base_rows, BF16),
         jnp.asarray(base_cols, BF16),
         jnp.asarray(turn_rows, F32),
+        jnp.asarray(turn_cols, F32),
     )
 
 
@@ -118,8 +123,8 @@
 
 
 def kernel(
-    shifts, mask, spec_h, diff_h, phases_h, trans_h, base_rows_h, base_cols_h, turn_rows_h, out_h,
-    spec, diff, phases, trans, wr, wc, turn_rows, out,
+    shifts, mask, spec_h, diff_h, phases_h, trans_h, base_rows_h, base_cols_h, turn_rows_h, turn_cols_h, out_h,
+    spec, diff, phases, trans, wr, wc, turn_rows, turn_cols, out,
     low0, high0, dw, trig0, trig1, pick_cols, pick_rows, back_rows, tspace,
     work_b, work_z, work_y, work_r, work_d, work_s, work_x, work_o,
     sa1, rb1, sm1, rd1, sm2, rb2, sb2, ra3, low1, high1, sa3, rb3, sm3, rd3, fs, rf, ts, tr,
@@ -170,7 +175,7 @@
     for at, (name, src, dst) in enumerate((
         ("diff", diff_h, diff), ("phases", phases_h, phases), ("spec", spec_h, spec),
         ("wr", base_rows_h, wr), ("turn_rows", turn_rows_h, turn_rows), ("trans", trans_h, trans),
-        ("wc", base_cols_h, wc),
+        ("wc", base_cols_h, wc), ("turn_cols", turn_cols_h, turn_cols),
     )):
         loads[name] = pltpu.make_async_copy(src, dst, in_sem.at[at])
         loads[name].start()
@@ -288,8 +293,8 @@
         high1[...] = jnp.zeros_like(high1)
 
     pl.semaphore_wait(barrier, 4)
-    for h in range(2):
-        halo_start(spec_h.at[:, :, pl.ds(256 * h, 256)], low0.at[h], high0.at[h], h)
+    for h in range(CHUNKS):
+        halo_start(spec_h.at[:, :, pl.ds(128 * h, 128)], low0.at[h], high0.at[h], h)
     tell(0)
     loads["phases"].wait()
 
@@ -309,20 +314,18 @@
     lax.fori_loop(6, 8, phase0, 0)
     loads["spec"].wait()
 
-    for h in range(2):
+    for h in range(CHUNKS):
         halo_wait(low0.at[h], high0.at[h], h)
-        for part in range(2):
-            cols = slice(256 * h + 128 * part, 256 * h + 128 * part + 128)
-            here = slice(128 * part, 128 * part + 128)
-            total = dot(dw[0, 1], spec[:, :, cols].reshape(512, 128))
-            total = total + dot(dw[0, 0], low0[h, :, :, here].reshape(512, 128))
-            total = total + dot(dw[0, 2], high0[h, :, :, here].reshape(512, 128))
-            cosine, sine = trig0[0, :, cols], trig0[1, :, cols]
-            real, imag = total[:256], total[256:]
-            wave_re = (real * cosine - imag * sine).astype(BF16)
-            wave_im = (real * sine + imag * cosine).astype(BF16)
-            sa1[h, 8 * part:8 * part + 8, :, 0:256] = wave_re.T.reshape(8, 16, 256)
-            sa1[h, 8 * part:8 * part + 8, :, 256:512] = wave_im.T.reshape(8, 16, 256)
+        cols = slice(128 * h, 128 * h + 128)
+        total = dot(dw[0, 1], spec[:, :, cols].reshape(512, 128))
+        total = total + dot(dw[0, 0], low0[h].reshape(512, 128))
+        total = total + dot(dw[0, 2], high0[h].reshape(512, 128))
+        cosine, sine = trig0[0, :, cols], trig0[1, :, cols]
+        real, imag = total[:256], total[256:]
+        wave_re = (real * cosine - imag * sine).astype(BF16)
+        wave_im = (real * sine + imag * cosine).astype(BF16)
+        sa1[h, :, :, 0:256] = wave_re.T.reshape(NR, 8, 256)
+        sa1[h, :, :, 256:512] = wave_im.T.reshape(NR, 8, 256)
         if h == 0:
             told(2)
             tell(3)
@@ -347,7 +350,7 @@
     told(5)
     cols_exchange(ts, tr, 0)
 
-    for name in ("wr", "wc", "turn_rows"):
+    for name in ("wr", "wc", "turn_rows", "turn_cols"):
         loads[name].wait()
 
     lane128 = iota((1, 128), 1)
@@ -380,20 +383,21 @@
             for r in range(NR):
                 real, imag = values[r]
                 cosine, sine = turn_rows[0, r, :, re], turn_rows[1, r, :, re]
-                work_b[r, :, re] = (real * cosine - imag * sine).astype(BF16)
-                work_b[r, :, im] = (real * sine + imag * cosine).astype(BF16)
+                work_b[r, :, re] = real * cosine - imag * sine
+                work_b[r, :, im] = real * sine + imag * cosine
             return 0
 
         lax.fori_loop(0, 2, first, 0)
+        rows = work_b[...].astype(BF16).reshape(128, 512)
         for part in range(2):
             lanes = slice(256 * part, 256 * part + 256)
-            got = dot(work_b[...].reshape(256, 512), wr[:, lanes])
-            work_z[:, 16 * h:16 * h + 16, lanes] = got.astype(BF16).reshape(NR, 16, 256)
+            got = dot(rows, wr[:, lanes])
+            work_z[:, 8 * h:8 * h + 8, lanes] = got.reshape(NR, 8, 256)
 
     def to_cols(send, recv, at):
         for half in range(2):
             def turn(g, _):
-                block = work_z[2 * g + half]
+                block = work_z[2 * g + half].astype(BF16)
                 block = jnp.concatenate([block[:, 128 * u:128 * u + 128] for u in range(4)], axis=0)
                 send[half, g] = block.T.reshape(NR, 8, 128)
                 return 0
@@ -413,7 +417,7 @@
                 values = butterfly([(work_x[u, 0, p], work_x[u, 1, p]) for p in range(NR)], 1)
                 for r in range(NR):
                     real, imag = values[r]
-                    cosine, sine = turn_rows[0, r, :, lanes], turn_rows[1, r, :, lanes]
+                    cosine, sine = turn_cols[0, r, :, lanes], turn_cols[1, r, :, lanes]
                     rows = slice(8 * u, 8 * u + 8)
                     work_d[r, rows, lanes] = real * cosine - imag * sine
                     work_d[r, rows, lanes2] = real * sine + imag * cosine
@@ -428,10 +432,10 @@
         trig1[1, cols, :] = sine.T
         return 0
 
-    for h in range(2):
+    for h in range(CHUNKS):
         arrived(rb1.at[h], 1 + h)
         forward_rows(rb1.at[h], h)
-    to_cols(sm1, rd1, 3)
+    to_cols(sm1, rd1, 5)
 
     lax.fori_loop(0, 4, phase1, 0)
     banded(1)
@@ -445,7 +449,7 @@
                 tspace[:, 4 * q + k, :, 128 * e:128 * e + 128] = got[k].reshape(2, 16, 128)
 
     for half in range(2):
-        arrived(rd1.at[half], 3 + half)
+        arrived(rd1.at[half], 5 + half)
         forward_cols(rd1.at[half])
         rows = work_d[...].astype(BF16).reshape(256, 512)
         for part in range(2):
@@ -463,7 +467,7 @@
                 values = []
                 for r in range(NR):
                     real, imag = work_d[r, 8 * u:8 * u + 8, re], work_d[r, 8 * u:8 * u + 8, im]
-                    cosine, sine = turn_rows[0, r, :, re], turn_rows[1, r, :, re]
+                    cosine, sine = turn_cols[0, r, :, re], turn_cols[1, r, :, re]
                     values.append((real * cosine + imag * sine, imag * cosine - real * sine))
                 values = butterfly(values, -1)
                 for r in range(NR):
@@ -475,10 +479,10 @@
             return 0
 
         lax.fori_loop(0, 2, last_cols, 0)
-        tiles_exchange(sm2.at[half], rb2.at[half], 11 + half)
+        tiles_exchange(sm2.at[half], rb2.at[half], 7 + half)
 
     for half in range(2):
-        arrived(rb2.at[half], 11 + half)
+        arrived(rb2.at[half], 7 + half)
 
         def untile(g, _):
             block = rb2[half, g].reshape(128, 128).T
@@ -491,8 +495,8 @@
             lanes = slice(256 * part, 256 * part + 256)
             got = dot_nt(work_y[...].reshape(256, 512), wr[lanes, :])
             work_r[half, :, :, lanes] = got.reshape(NC, 32, 256)
-    for h in range(2):
-        crow = slice(16 * h, 16 * h + 16)
+    for h in range(CHUNKS):
+        crow = slice(8 * h, 8 * h + 8)
 
         def sources(at, _):
             half = pl.multiple_of(at * 128, 128)
@@ -509,29 +513,29 @@
             return 0
 
         lax.fori_loop(0, 2, sources, 0)
-        rows_exchange(sb2.at[h], ra3.at[h], 5 + h)
-
-    for h in range(2):
-        arrived(ra3.at[h], 5 + h)
-        halo_start(ra3.at[h], low1.at[h], high1.at[h], 2 + h)
-
-    for h in range(2):
-        halo_wait(low1.at[h], high1.at[h], 2 + h)
-        total = dot_nt(ra3[h].reshape(256, 512), dw[1, 1])
-        total = total + dot_nt(low1[h].reshape(256, 512), dw[1, 0])
-        total = total + dot_nt(high1[h].reshape(256, 512), dw[1, 2])
-        rows = slice(256 * h, 256 * h + 256)
+        rows_exchange(sb2.at[h], ra3.at[h], 9 + h)
+
+    for h in range(CHUNKS):
+        arrived(ra3.at[h], 9 + h)
+        halo_start(ra3.at[h], low1.at[h], high1.at[h], CHUNKS + h)
+
+    for h in range(CHUNKS):
+        halo_wait(low1.at[h], high1.at[h], CHUNKS + h)
+        total = dot_nt(ra3[h].reshape(128, 512), dw[1, 1])
+        total = total + dot_nt(low1[h].reshape(128, 512), dw[1, 0])
+        total = total + dot_nt(high1[h].reshape(128, 512), dw[1, 2])
+        rows = slice(128 * h, 128 * h + 128)
         cosine, sine = trig1[0, rows, :], trig1[1, rows, :]
         real, imag = total[:, :256], total[:, 256:]
-        sa3[h, :, :, 0:256] = (real * cosine - imag * sine).astype(BF16).reshape(NR, 16, 256)
-        sa3[h, :, :, 256:512] = (real * sine + imag * cosine).astype(BF16).reshape(NR, 16, 256)
-        rows_exchange(sa3.at[h], rb3.at[h], 7 + h)
-    for h in range(2):
-        arrived(rb3.at[h], 7 + h)
+        sa3[h, :, :, 0:256] = (real * cosine - imag * sine).astype(BF16).reshape(NR, 8, 256)
+        sa3[h, :, :, 256:512] = (real * sine + imag * cosine).astype(BF16).reshape(NR, 8, 256)
+        rows_exchange(sa3.at[h], rb3.at[h], 13 + h)
+    for h in range(CHUNKS):
+        arrived(rb3.at[h], 13 + h)
         forward_rows(rb3.at[h], h)
-    to_cols(sm3, rd3, 9)
+    to_cols(sm3, rd3, 17)
     for half in range(2):
-        arrived(rd3.at[half], 9 + half)
+        arrived(rd3.at[half], 17 + half)
         forward_cols(rd3.at[half])
         rows = work_d[...].astype(BF16).reshape(256, 512)
         for plane in range(2):
@@ -544,9 +548,9 @@
                     got = crossed([work_d[4 * q + k, :, src] for k in range(4)])
                     for k in range(4):
                         fs[half, 4 * e + k, :, lanes_to] = got[k].astype(BF16)
-        cols_exchange(fs.at[half], rf.at[half], 13 + half)
+        cols_exchange(fs.at[half], rf.at[half], 19 + half)
     for half in range(2):
-        arrived(rf.at[half], 13 + half)
+        arrived(rf.at[half], 19 + half)
         for plane in range(2):
             lanes = slice(512 * plane, 512 * plane + 512)
             ordered = dot_nt(rf[half, :, :, lanes].reshape(128, 512), pick_cols[...])
@@ -569,7 +573,7 @@
     def vmem(kind, *shape):
         return pltpu.VMEM(shape, kind)
 
-    halves = (2, NR, 16, 512)
+    halves = (CHUNKS, NR, 8, 512)
     space = pl.pallas_call(
         kernel,
         out_shape=jax.ShapeDtypeStruct((2, 256, 512), BF16),
@@ -577,14 +581,14 @@
         out_specs=anywhere,
         scratch_shapes=[pltpu.VMEM(x.shape, x.dtype) for x in operands] + [
             vmem(BF16, 2, 256, 512),
-            vmem(BF16, 2, 2, 256, 256), vmem(BF16, 2, 2, 256, 256),
+            vmem(BF16, CHUNKS, 2, 256, 128), vmem(BF16, CHUNKS, 2, 256, 128),
             vmem(BF16, 2, 3, 512, 512),
             vmem(F32, 2, 256, 512),
             vmem(F32, 2, 512, 256),
             vmem(BF16, 512, 512), vmem(BF16, 256, 256), vmem(BF16, 256, 256),
             vmem(F32, 2, NR, 16, 256),
-            vmem(BF16, NR, 16, 512),
-            vmem(BF16, NR, 32, 512),
+            vmem(F32, NR, 8, 512),
+            vmem(F32, NR, 32, 512),
             vmem(BF16, NC, 32, 512),
             vmem(F32, 2, NC, 32, 512),
             vmem(F32, NR, 16, 512),
@@ -601,9 +605,9 @@
             vmem(BF16, 2, NC, 16, 1024), vmem(BF16, 2, NC, 16, 1024),
             vmem(BF16, NC, 2, 16, 512), vmem(BF16, NC, 2, 16, 512),
             pltpu.SemaphoreType.DMA((11,)),
-            pltpu.SemaphoreType.DMA((15,)),
-            pltpu.SemaphoreType.DMA((15,)),
-            pltpu.SemaphoreType.DMA((4, 4)),
+            pltpu.SemaphoreType.DMA((21,)),
+            pltpu.SemaphoreType.DMA((21,)),
+            pltpu.SemaphoreType.DMA((2 * CHUNKS, 4)),
             pltpu.SemaphoreType.REGULAR((6,)),
         ],
         compiler_params=pltpu.CompilerParams(

time: 90.1 us -> 89 us (0.988)
  Pallas kernels: 87.7 us -> 86.6 us
    pallas_call x1, Pallas kernels: 87.7 us -> 86.6 us  [on_device(): pl.pallas_call(kernel, out_shape=jax.ShapeDtypeStruct((2, 256, 512), BF16...]
where the time goes in v6:
time: 89 us; the launch traced here: 88.8 us
  Pallas kernels  86.6 us (97%)
  other arithmetic  2.17 us (2%)
    pallas_call x1, Pallas kernels, on_device(): pl.pallas_call(kernel, out_shape=jax.ShapeDtypeStruct((2, 256, 512), BF16...  86.6 us
    mul x1, other arithmetic, on_device(): return space.astype(F32) * transmission[None]  2.17 us

profile of v6, /device:TPU:1, one launch (start us, length us, event | category | flops | bytes accessed | tf_op | source)
XLA Modules:
  0.0 88.8 jit_solution(7522691723120541010)
XLA Ops:
  0.0 0.0 copy-start
  0.0 86.6 %shard_map.100 = bf16[2,256,512]{2,1,0:T(8,128)(2,1)} custom-call(s32[2]{0:T(128)} %shifts.1, s32[2,3]{1,0:T(2,128)} %mask.1, bf16[2,256,512]{2,1,0:T(8,128)(2,1)} %spec_h.1, bf16[2,2,3,128,128]{4,3,2,1,0:T(8,128)(2,1)} %diff_h.1, f32[2,256,512]{2,1,0:T(8,128)} %phases_h.1, f32[256,512]{1,0:T(8,128)} %trans_h.1, bf16[512,512]{1,0:T(8,128)(2,1)} %constant.8.clone.base_rows_h, ...), custom_call_target="tpu_custom_call" | custom-call | tf_op jit(solution)/shard_map/pallas_call | solution.py:577
  86.6 0.0 copy-done
  86.6 2.2 %convert_multiply_fusion = f32[2,256,512]{2,1,0:T(8,128)} fusion(bf16[2,256,512]{2,1,0:T(8,128)(2,1)} %shard_map.100, f32[256,512]{1,0:T(8,128)S(1)} %copy-done), kind=kLoop, calls=%fused_computation | loop fusion | flops 524288 | bytes 2097152 | tf_op jit(solution)/shard_map/mul | solution.py:617
Async XLA Ops:
  0.0 86.6 %copy-start = (f32[256,512]{1,0:T(8,128)S(1)}, f32[256,512]{1,0:T(8,128)}, u32[]{:S(2)}) copy-start(f32[256,512]{1,0:T(8,128)} %trans_h.1) | copy-start | bytes 1572868

commit v7 on v6

--- a/solution.py
+++ b/solution.py
@@ -126,7 +126,7 @@
     shifts, mask, spec_h, diff_h, phases_h, trans_h, base_rows_h, base_cols_h, turn_rows_h, turn_cols_h, out_h,
     spec, diff, phases, trans, wr, wc, turn_rows, turn_cols, out,
     low0, high0, dw, trig0, trig1, pick_cols, pick_rows, back_rows, tspace,
-    work_b, work_z, work_y, work_r, work_d, work_s, work_x, work_o,
+    work_b, work_z, work_y, work_r, work_d, work_s, work_x, work_o, own0, own1,
     sa1, rb1, sm1, rd1, sm2, rb2, sb2, ra3, low1, high1, sa3, rb3, sm3, rd3, fs, rf, ts, tr,
     in_sem, send_sem, recv_sem, halo_sem, ready_sem,
 ):
@@ -203,6 +203,9 @@
         for row_step, col_step in PAIR_STEPS[:-1]:
             d, g = row_peer[row_step], col_peer[col_step]
             remote(src.at[g, d], dst.at[cp, rp], at, {"rows": d, "cols": g}).start()
+        tiles_kept(src, dst, at)
+
+    def tiles_kept(src, dst, at):
         pltpu.make_async_copy(src.at[cp, rp], dst.at[cp, rp], recv_sem.at[at]).start()
         waits.append(lambda: sent(src.at[pl.ds(0, NC - 1)], at))
         waits.append(lambda: sent(src.at[0, pl.ds(0, NR - 1)], at))
@@ -315,10 +318,11 @@
     loads["spec"].wait()
 
     for h in range(CHUNKS):
+        own0[h] = dot(dw[0, 1], spec[:, :, 128 * h:128 * h + 128].reshape(512, 128))
+    for h in range(CHUNKS):
         halo_wait(low0.at[h], high0.at[h], h)
         cols = slice(128 * h, 128 * h + 128)
-        total = dot(dw[0, 1], spec[:, :, cols].reshape(512, 128))
-        total = total + dot(dw[0, 0], low0[h].reshape(512, 128))
+        total = own0[h] + dot(dw[0, 0], low0[h].reshape(512, 128))
         total = total + dot(dw[0, 2], high0[h].reshape(512, 128))
         cosine, sine = trig0[0, :, cols], trig0[1, :, cols]
         real, imag = total[:256], total[256:]
@@ -396,14 +400,22 @@
 
     def to_cols(send, recv, at):
         for half in range(2):
-            def turn(g, _):
+            def turn(g):
                 block = work_z[2 * g + half].astype(BF16)
                 block = jnp.concatenate([block[:, 128 * u:128 * u + 128] for u in range(4)], axis=0)
                 send[half, g] = block.T.reshape(NR, 8, 128)
-                return 0
-
-            lax.fori_loop(0, NC, turn, 0)
-            tiles_exchange(send.at[half], recv.at[half], at + half)
+
+            turn(col_peer[COL_STEPS[0]])
+            for number, col_step in enumerate(COL_STEPS):
+                if number < NC - 1:
+                    turn(col_peer[COL_STEPS[number + 1]])
+                g = col_peer[col_step]
+                for row_step in ROW_STEPS:
+                    d = row_peer[row_step]
+                    if any(row_step) or any(col_step):
+                        device = {"rows": d, "cols": g}
+                        remote(send.at[half, g, d], recv.at[half, cp, rp], at + half, device).start()
+            tiles_kept(send.at[half], recv.at[half], at + half)
 
     def forward_cols(src):
         def first(at, _):
@@ -518,11 +530,11 @@
     for h in range(CHUNKS):
         arrived(ra3.at[h], 9 + h)
         halo_start(ra3.at[h], low1.at[h], high1.at[h], CHUNKS + h)
+        own1[h] = dot_nt(ra3[h].reshape(128, 512), dw[1, 1])
 
     for h in range(CHUNKS):
         halo_wait(low1.at[h], high1.at[h], CHUNKS + h)
-        total = dot_nt(ra3[h].reshape(128, 512), dw[1, 1])
-        total = total + dot_nt(low1[h].reshape(128, 512), dw[1, 0])
+        total = own1[h] + dot_nt(low1[h].reshape(128, 512), dw[1, 0])
         total = total + dot_nt(high1[h].reshape(128, 512), dw[1, 2])
         rows = slice(128 * h, 128 * h + 128)
         cosine, sine = trig1[0, rows, :], trig1[1, rows, :]
@@ -595,6 +607,7 @@
             vmem(BF16, 256, 512),
             vmem(F32, 2, 2, NR, 8, 128),
             vmem(BF16, 2, 256, 512),
+            vmem(F32, CHUNKS, 512, 128), vmem(F32, CHUNKS, 128, 512),
             vmem(BF16, *halves), vmem(BF16, *halves),
             vmem(BF16, 2, NC, NR, 8, 128), vmem(BF16, 2, NC, NR, 8, 128),
             vmem(BF16, 2, NC, NR, 8, 128), vmem(BF16, 2, NC, NR, 8, 128),

time: 89 us -> 88.3 us (level)
  no operation moved by 1% of the time
where the time goes in v7:
time: 88.3 us; the launch traced here: 88.1 us
  Pallas kernels  85.9 us (97%)
  other arithmetic  2.17 us (2%)
    pallas_call x1, Pallas kernels, on_device(): pl.pallas_call(kernel, out_shape=jax.ShapeDtypeStruct((2, 256, 512), BF16...  85.9 us
    mul x1, other arithmetic, on_device(): return space.astype(F32) * transmission[None]  2.17 us

profile of v7, /device:TPU:1, one launch (start us, length us, event | category | flops | bytes accessed | tf_op | source)
XLA Modules:
  0.0 88.1 jit_solution(18005556225171439378)
XLA Ops:
  0.0 0.0 copy-start
  0.0 85.9 %shard_map.100 = bf16[2,256,512]{2,1,0:T(8,128)(2,1)} custom-call(s32[2]{0:T(128)} %shifts.1, s32[2,3]{1,0:T(2,128)} %mask.1, bf16[2,256,512]{2,1,0:T(8,128)(2,1)} %spec_h.1, bf16[2,2,3,128,128]{4,3,2,1,0:T(8,128)(2,1)} %diff_h.1, f32[2,256,512]{2,1,0:T(8,128)} %phases_h.1, f32[256,512]{1,0:T(8,128)} %trans_h.1, bf16[512,512]{1,0:T(8,128)(2,1)} %constant.8.clone.base_rows_h, ...), custom_call_target="tpu_custom_call" | custom-call | tf_op jit(solution)/shard_map/pallas_call | solution.py:589
  85.9 0.0 copy-done
  85.9 2.2 %convert_multiply_fusion = f32[2,256,512]{2,1,0:T(8,128)} fusion(bf16[2,256,512]{2,1,0:T(8,128)(2,1)} %shard_map.100, f32[256,512]{1,0:T(8,128)S(1)} %copy-done), kind=kLoop, calls=%fused_computation | loop fusion | flops 524288 | bytes 2097152 | tf_op jit(solution)/shard_map/mul | solution.py:630
Async XLA Ops:
  0.0 85.9 %copy-start = (f32[256,512]{1,0:T(8,128)S(1)}, f32[256,512]{1,0:T(8,128)}, u32[]{:S(2)}) copy-start(f32[256,512]{1,0:T(8,128)} %trans_h.1) | copy-start | bytes 1572868

commit v8 on v7

--- a/solution.py
+++ b/solution.py
@@ -199,12 +199,6 @@
         pltpu.make_async_copy(src.at[cp], dst.at[cp], recv_sem.at[at]).start()
         waits.append(lambda: sent(src.at[pl.ds(0, NC - 1)], at))
 
-    def tiles_exchange(src, dst, at):
-        for row_step, col_step in PAIR_STEPS[:-1]:
-            d, g = row_peer[row_step], col_peer[col_step]
-            remote(src.at[g, d], dst.at[cp, rp], at, {"rows": d, "cols": g}).start()
-        tiles_kept(src, dst, at)
-
     def tiles_kept(src, dst, at):
         pltpu.make_async_copy(src.at[cp, rp], dst.at[cp, rp], recv_sem.at[at]).start()
         waits.append(lambda: sent(src.at[pl.ds(0, NC - 1)], at))
@@ -472,7 +466,7 @@
             lanes = slice(256 * part, 256 * part + 256)
             work_d[:, :, lanes] = dot_nt(work_s[...], wc[lanes, :]).reshape(NR, 16, 256)
 
-        def last_cols(at, _):
+        def last_cols(at):
             re = pl.ds(pl.multiple_of(at * 128, 128), 128)
             im = pl.ds(pl.multiple_of(at * 128 + 256, 128), 128)
             for u in range(2):
@@ -488,10 +482,15 @@
                 tiles = crossed([work_x[k // 4, k // 2 % 2, 2 * q + k % 2] for k in range(8)])
                 for low in range(8):
                     sm2[half, q, at * 8 + low] = tiles[low].astype(BF16)
-            return 0
-
-        lax.fori_loop(0, 2, last_cols, 0)
-        tiles_exchange(sm2.at[half], rb2.at[half], 7 + half)
+
+        for other in (1, 0):
+            last_cols(lax.rem(z_lo + other, 2))
+            for row_step, col_step in PAIR_STEPS[:-1]:
+                if row_step[0] == other:
+                    d, g = row_peer[row_step], col_peer[col_step]
+                    device = {"rows": d, "cols": g}
+                    remote(sm2.at[half, g, d], rb2.at[half, cp, rp], 7 + half, device).start()
+        tiles_kept(sm2.at[half], rb2.at[half], 7 + half)
 
     for half in range(2):
         arrived(rb2.at[half], 7 + half)
@@ -567,11 +566,11 @@
             lanes = slice(512 * plane, 512 * plane + 512)
             ordered = dot_nt(rf[half, :, :, lanes].reshape(128, 512), pick_cols[...])
             work_o[plane, 128 * half:128 * half + 128, :] = ordered.astype(BF16)
-    for plane in range(2):
-        out[plane] = dot(back_rows[...], work_o[plane]).astype(BF16)
-        result = pltpu.make_async_copy(out.at[plane], out_h.at[plane], in_sem.at[9 + plane])
-        result.start()
-        waits.append(result.wait)
+            if half == 1:
+                out[plane] = dot(back_rows[...], work_o[plane]).astype(BF16)
+                result = pltpu.make_async_copy(out.at[plane], out_h.at[plane], in_sem.at[9 + plane])
+                result.start()
+                waits.append(result.wait)
 
     finish()
 
@@ -624,7 +623,7 @@
             pltpu.SemaphoreType.REGULAR((6,)),
         ],
         compiler_params=pltpu.CompilerParams(
-            collective_id=0, has_side_effects=True, vmem_limit_bytes=60 * 1024 * 1024
+            collective_id=0, has_side_effects=True, vmem_limit_bytes=40 * 1024 * 1024
         ),
     )(shifts, order_mask, *operands)
     return space.astype(F32) * transmission[None]

time: 88.3 us -> 95.7 us (1.084)
  local copies, waits for them, and re-layouts: 0.01 us -> 9.23 us
  Pallas kernels: 85.9 us -> 84.8 us
  other arithmetic: 2.17 us -> 1.12 us
    unnamed x2 -> x20, local copies, waits for them, and re-layouts: 0.01 us -> 9.23 us
    pallas_call x1, Pallas kernels: 85.9 us -> 84.8 us  [on_device(): pl.pallas_call(kernel, out_shape=jax.ShapeDtypeStruct((2, 256, 512), BF16...]
    mul x1, other arithmetic: 2.17 us -> 1.12 us  [on_device(): return space.astype(F32) * transmission[None]]
where the time goes in v8:
time: 95.7 us; the launch traced here: 95.2 us
  Pallas kernels  84.8 us (89%)
  local copies, waits for them, and re-layouts  9.23 us (10%)
  other arithmetic  1.12 us (1%)
    pallas_call x1, Pallas kernels, on_device(): pl.pallas_call(kernel, out_shape=jax.ShapeDtypeStruct((2, 256, 512), BF16...  84.8 us
    unnamed x20, local copies, waits for them, and re-layouts  9.23 us

profile of v8, /device:TPU:1, one launch (start us, length us, event | category | flops | bytes accessed | tf_op | source)
XLA Modules:
  0.0 95.2 jit_solution(9393311827291512885)
XLA Ops:
  0.0 0.0 copy-start
  0.0 1.0 %copy-done = f32[256,512]{1,0:T(8,128)S(1)} copy-done((f32[256,512]{1,0:T(8,128)S(1)}, f32[256,512]{1,0:T(8,128)}, u32[]{:S(2)}) %copy-start) | copy-done | bytes 524312
  1.0 0.0 copy-start.1
  1.0 1.2 %copy-done.1 = f32[2,256,512]{2,1,0:T(8,128)S(1)} copy-done((f32[2,256,512]{2,1,0:T(8,128)S(1)}, f32[2,256,512]{2,1,0:T(8,128)}, u32[]{:S(2)}) %copy-start.1) | copy-done | bytes 1048600
  2.3 0.0 copy-start.2
  2.3 1.0 %copy-done.2 = bf16[2,256,512]{2,1,0:T(8,128)(2,1)S(1)} copy-done((bf16[2,256,512]{2,1,0:T(8,128)(2,1)S(1)}, bf16[2,256,512]{2,1,0:T(8,128)(2,1)}, u32[]{:S(2)}) %copy-start.2) | copy-done | bytes 524312
  3.3 0.0 copy-start.3
  3.3 1.0 %copy-done.3 = bf16[512,512]{1,0:T(8,128)(2,1)S(1)} copy-done((bf16[512,512]{1,0:T(8,128)(2,1)S(1)}, bf16[512,512]{1,0:T(8,128)(2,1)}, u32[]{:S(2)}) %copy-start.3) | copy-done | bytes 524312
  4.4 0.0 copy-start.4
  4.4 1.0 %copy-done.4 = bf16[512,512]{1,0:T(8,128)(2,1)S(1)} copy-done((bf16[512,512]{1,0:T(8,128)(2,1)S(1)}, bf16[512,512]{1,0:T(8,128)(2,1)}, u32[]{:S(2)}) %copy-start.4) | copy-done | bytes 524312
  5.4 0.0 copy-start.5
  5.4 1.0 %copy-done.5 = bf16[2,2,3,128,128]{4,3,2,1,0:T(8,128)(2,1)S(1)} copy-done((bf16[2,2,3,128,128]{4,3,2,1,0:T(8,128)(2,1)S(1)}, bf16[2,2,3,128,128]{4,3,2,1,0:T(8,128)(2,1)}, u32[]{:S(2)}) %copy-start.5) | copy-done | bytes 393240
  6.4 0.0 copy-start.6
  6.4 0.8 copy-done.6
  7.1 0.0 copy-start.7
  7.2 0.8 copy-done.7
  7.9 0.0 copy-start.8
  7.9 0.7 copy-done.8
  8.6 0.0 copy-start.9
  8.6 0.7 copy-done.9
  9.2 84.8 %shard_map.100 = bf16[2,256,512]{2,1,0:T(8,128)(2,1)S(1)} custom-call(s32[2]{0:T(128)S(1)} %copy-done.9, s32[2,3]{1,0:T(2,128)S(1)} %copy-done.8, bf16[2,256,512]{2,1,0:T(8,128)(2,1)S(1)} %copy-done.2, bf16[2,2,3,128,128]{4,3,2,1,0:T(8,128)(2,1)S(1)} %copy-done.5, f32[2,256,512]{2,1,0:T(8,128)S(1)} %copy-done.1, f32[256,512]{1,0:T(8,128)S(1)} %copy-done, ...), custom_call_target="tpu_custom_call" | custom-call | tf_op jit(solution)/shard_map/pallas_call | solution.py:588
  94.1 1.1 %convert_multiply_fusion = f32[2,256,512]{2,1,0:T(8,128)} fusion(bf16[2,256,512]{2,1,0:T(8,128)(2,1)S(1)} %shard_map.100, f32[256,512]{1,0:T(8,128)S(1)} %copy-done), kind=kLoop, calls=%fused_computation | loop fusion | flops 524288 | bytes 2097152 | tf_op jit(solution)/shard_map/mul | solution.py:629
Async XLA Ops:
  0.0 1.0 %copy-start = (f32[256,512]{1,0:T(8,128)S(1)}, f32[256,512]{1,0:T(8,128)}, u32[]{:S(2)}) copy-start(f32[256,512]{1,0:T(8,128)} %trans_h.1) | copy-start | bytes 1572868
  1.0 1.2 %copy-start.1 = (f32[2,256,512]{2,1,0:T(8,128)S(1)}, f32[2,256,512]{2,1,0:T(8,128)}, u32[]{:S(2)}) copy-start(f32[2,256,512]{2,1,0:T(8,128)} %phases_h.1) | copy-start | bytes 3145732
  2.3 1.0 %copy-start.2 = (bf16[2,256,512]{2,1,0:T(8,128)(2,1)S(1)}, bf16[2,256,512]{2,1,0:T(8,128)(2,1)}, u32[]{:S(2)}) copy-start(bf16[2,256,512]{2,1,0:T(8,128)(2,1)} %spec_h.1) | copy-start | bytes 1572868
  3.3 1.0 %copy-start.3 = (bf16[512,512]{1,0:T(8,128)(2,1)S(1)}, bf16[512,512]{1,0:T(8,128)(2,1)}, u32[]{:S(2)}) copy-start(bf16[512,512]{1,0:T(8,128)(2,1)} %constant.9.clone.base_cols_h) | copy-start | bytes 1572868
  4.4 1.0 %copy-start.4 = (bf16[512,512]{1,0:T(8,128)(2,1)S(1)}, bf16[512,512]{1,0:T(8,128)(2,1)}, u32[]{:S(2)}) copy-start(bf16[512,512]{1,0:T(8,128)(2,1)} %constant.8.clone.base_rows_h) | copy-start | bytes 1572868
  5.4 1.0 %copy-start.5 = (bf16[2,2,3,128,128]{4,3,2,1,0:T(8,128)(2,1)S(1)}, bf16[2,2,3,128,128]{4,3,2,1,0:T(8,128)(2,1)}, u32[]{:S(2)}) copy-start(bf16[2,2,3,128,128]{4,3,2,1,0:T(8,128)(2,1)} %diff_h.1) | copy-start | bytes 1179652
  6.4 0.8 copy-start.6
  7.1 0.8 copy-start.7
  7.9 0.7 copy-start.8
  8.6 0.7 copy-start.9

commit v9 on v8

--- a/solution.py
+++ b/solution.py
@@ -467,8 +467,7 @@
             work_d[:, :, lanes] = dot_nt(work_s[...], wc[lanes, :]).reshape(NR, 16, 256)
 
         def last_cols(at):
-            re = pl.ds(pl.multiple_of(at * 128, 128), 128)
-            im = pl.ds(pl.multiple_of(at * 128 + 256, 128), 128)
+            re, im = slice(128 * at, 128 * at + 128), slice(128 * at + 256, 128 * at + 384)
             for u in range(2):
                 values = []
                 for r in range(NR):
@@ -483,13 +482,11 @@
                 for low in range(8):
                     sm2[half, q, at * 8 + low] = tiles[low].astype(BF16)
 
-        for other in (1, 0):
-            last_cols(lax.rem(z_lo + other, 2))
-            for row_step, col_step in PAIR_STEPS[:-1]:
-                if row_step[0] == other:
-                    d, g = row_peer[row_step], col_peer[col_step]
-                    device = {"rows": d, "cols": g}
-                    remote(sm2.at[half, g, d], rb2.at[half, cp, rp], 7 + half, device).start()
+        for at in range(2):
+            last_cols(at)
+        for row_step, col_step in PAIR_STEPS[:-1]:
+            d, g = row_peer[row_step], col_peer[col_step]
+            remote(sm2.at[half, g, d], rb2.at[half, cp, rp], 7 + half, {"rows": d, "cols": g}).start()
         tiles_kept(sm2.at[half], rb2.at[half], 7 + half)
 
     for half in range(2):

time: 95.7 us -> 95.9 us (level)
  no operation moved by 1% of the time
where the time goes in v9:
time: 95.9 us; the launch traced here: 95.3 us
  Pallas kernels  85 us (89%)
  local copies, waits for them, and re-layouts  9.23 us (10%)
  other arithmetic  1.12 us (1%)
    pallas_call x1, Pallas kernels, on_device(): pl.pallas_call(kernel, out_shape=jax.ShapeDtypeStruct((2, 256, 512), BF16...  85 us
    unnamed x20, local copies, waits for them, and re-layouts  9.23 us

profile of v9, /device:TPU:1, one launch (start us, length us, event | category | flops | bytes accessed | tf_op | source)
XLA Modules:
  0.0 95.3 jit_solution(8864801392740758669)
XLA Ops:
  0.0 0.0 copy-start
  0.0 1.0 %copy-done = f32[256,512]{1,0:T(8,128)S(1)} copy-done((f32[256,512]{1,0:T(8,128)S(1)}, f32[256,512]{1,0:T(8,128)}, u32[]{:S(2)}) %copy-start) | copy-done | bytes 524312
  1.0 0.0 copy-start.1
  1.0 1.2 %copy-done.1 = f32[2,256,512]{2,1,0:T(8,128)S(1)} copy-done((f32[2,256,512]{2,1,0:T(8,128)S(1)}, f32[2,256,512]{2,1,0:T(8,128)}, u32[]{:S(2)}) %copy-start.1) | copy-done | bytes 1048600
  2.3 0.0 copy-start.2
  2.3 1.0 %copy-done.2 = bf16[2,256,512]{2,1,0:T(8,128)(2,1)S(1)} copy-done((bf16[2,256,512]{2,1,0:T(8,128)(2,1)S(1)}, bf16[2,256,512]{2,1,0:T(8,128)(2,1)}, u32[]{:S(2)}) %copy-start.2) | copy-done | bytes 524312
  3.3 0.0 copy-start.3
  3.3 1.0 %copy-done.3 = bf16[512,512]{1,0:T(8,128)(2,1)S(1)} copy-done((bf16[512,512]{1,0:T(8,128)(2,1)S(1)}, bf16[512,512]{1,0:T(8,128)(2,1)}, u32[]{:S(2)}) %copy-start.3) | copy-done | bytes 524312
  4.4 0.0 copy-start.4
  4.4 1.0 %copy-done.4 = bf16[512,512]{1,0:T(8,128)(2,1)S(1)} copy-done((bf16[512,512]{1,0:T(8,128)(2,1)S(1)}, bf16[512,512]{1,0:T(8,128)(2,1)}, u32[]{:S(2)}) %copy-start.4) | copy-done | bytes 524312
  5.4 0.0 copy-start.5
  5.4 1.0 %copy-done.5 = bf16[2,2,3,128,128]{4,3,2,1,0:T(8,128)(2,1)S(1)} copy-done((bf16[2,2,3,128,128]{4,3,2,1,0:T(8,128)(2,1)S(1)}, bf16[2,2,3,128,128]{4,3,2,1,0:T(8,128)(2,1)}, u32[]{:S(2)}) %copy-start.5) | copy-done | bytes 393240
  6.4 0.0 copy-start.6
  6.4 0.8 copy-done.6
  7.1 0.0 copy-start.7
  7.2 0.8 copy-done.7
  7.9 0.0 copy-start.8
  7.9 0.7 copy-done.8
  8.6 0.0 copy-start.9
  8.6 0.7 copy-done.9
  9.2 85.0 %shard_map.100 = bf16[2,256,512]{2,1,0:T(8,128)(2,1)S(1)} custom-call(s32[2]{0:T(128)S(1)} %copy-done.9, s32[2,3]{1,0:T(2,128)S(1)} %copy-done.8, bf16[2,256,512]{2,1,0:T(8,128)(2,1)S(1)} %copy-done.2, bf16[2,2,3,128,128]{4,3,2,1,0:T(8,128)(2,1)S(1)} %copy-done.5, f32[2,256,512]{2,1,0:T(8,128)S(1)} %copy-done.1, f32[256,512]{1,0:T(8,128)S(1)} %copy-done, ...), custom_call_target="tpu_custom_call" | custom-call | tf_op jit(solution)/shard_map/pallas_call | solution.py:585
  94.2 1.1 %convert_multiply_fusion = f32[2,256,512]{2,1,0:T(8,128)} fusion(bf16[2,256,512]{2,1,0:T(8,128)(2,1)S(1)} %shard_map.100, f32[256,512]{1,0:T(8,128)S(1)} %copy-done), kind=kLoop, calls=%fused_computation | loop fusion | flops 524288 | bytes 2097152 | tf_op jit(solution)/shard_map/mul | solution.py:626
Async XLA Ops:
  0.0 1.0 %copy-start = (f32[256,512]{1,0:T(8,128)S(1)}, f32[256,512]{1,0:T(8,128)}, u32[]{:S(2)}) copy-start(f32[256,512]{1,0:T(8,128)} %trans_h.1) | copy-start | bytes 1572868
  1.0 1.2 %copy-start.1 = (f32[2,256,512]{2,1,0:T(8,128)S(1)}, f32[2,256,512]{2,1,0:T(8,128)}, u32[]{:S(2)}) copy-start(f32[2,256,512]{2,1,0:T(8,128)} %phases_h.1) | copy-start | bytes 3145732
  2.3 1.0 %copy-start.2 = (bf16[2,256,512]{2,1,0:T(8,128)(2,1)S(1)}, bf16[2,256,512]{2,1,0:T(8,128)(2,1)}, u32[]{:S(2)}) copy-start(bf16[2,256,512]{2,1,0:T(8,128)(2,1)} %spec_h.1) | copy-start | bytes 1572868
  3.3 1.0 %copy-start.3 = (bf16[512,512]{1,0:T(8,128)(2,1)S(1)}, bf16[512,512]{1,0:T(8,128)(2,1)}, u32[]{:S(2)}) copy-start(bf16[512,512]{1,0:T(8,128)(2,1)} %constant.9.clone.base_cols_h) | copy-start | bytes 1572868
  4.4 1.0 %copy-start.4 = (bf16[512,512]{1,0:T(8,128)(2,1)S(1)}, bf16[512,512]{1,0:T(8,128)(2,1)}, u32[]{:S(2)}) copy-start(bf16[512,512]{1,0:T(8,128)(2,1)} %constant.8.clone.base_rows_h) | copy-start | bytes 1572868
  5.4 1.0 %copy-start.5 = (bf16[2,2,3,128,128]{4,3,2,1,0:T(8,128)(2,1)S(1)}, bf16[2,2,3,128,128]{4,3,2,1,0:T(8,128)(2,1)}, u32[]{:S(2)}) copy-start(bf16[2,2,3,128,128]{4,3,2,1,0:T(8,128)(2,1)} %diff_h.1) | copy-start | bytes 1179652
  6.4 0.8 copy-start.6
  7.1 0.8 copy-start.7
  7.9 0.7 copy-start.8
  8.6 0.7 copy-start.9
